TPU v7x, 256 devices: a whole 4x4x8 slice. The times are simulated.
256 devices in a mesh: gx: 8 (over y, core), gy: 32 (over z, x).
Axes of the slice: x: 4, y: 4, z: 8, core: 2. Of those that a mesh axis runs over, the one named last changes fastest.
Arguments:
- source: float32 [512, 2, 8, 2048], P('gy', None, None, 'gx'), may hold values from -6 to 6
- lower_coef: float32 [512], P('gy'), may hold values from 0.2 to 36
- upper_coef: float32 [512], P('gy'), may hold values from 0.2 to 36
- span_wave: float32 [8], replicated, may hold values from 0.01 to 0.04
Outputs:
- pressure: float32 [512, 2, 8, 2048], P('gy', None, None, 'gx')
All inputs are finite; a program needn't handle non-finite values.
Results may differ from a plain program's by a relative error of at most 0.00075.
Values sent between devices are 32-bit elements; how exact they have to be, the bound alone decides.
A program may use at most 64 MiB of HBM per device.

v0:
```python
import math

import jax
import jax.numpy as jnp
from jax import lax
from jax.sharding import Mesh
from jax.sharding import PartitionSpec as P

GY = ("gy_0", "gy_1")


exact_prec = lax.Precision.HIGHEST
full_turn = 2.0 * math.pi


def neutral_like(array, identity):
    return jax.tree.map(
        lambda a, e: jnp.broadcast_to(jnp.asarray(e, a.dtype), a.shape), array, identity
    )


def collected_together(array, axis):
    leaves = jax.tree.leaves(array)
    order = sorted(range(len(leaves)), key=lambda k: -leaves[k].size)
    width = (1, *leaves[order[0]].shape)[-1]
    lines = [
        jnp.pad(leaves[k].reshape(-1), (0, -leaves[k].size % width)).reshape(-1, width)
        for k in order
    ]
    both, at, found = (lax.all_gather(jnp.concatenate(lines), axis), 0, {})
    for k, line in zip(order, lines):
        share = both[:, at : at + len(line)].reshape(len(both), -1)
        found[k] = share[:, : leaves[k].size].reshape(-1, *leaves[k].shape)
        at += len(line)
    numbers = iter(range(len(leaves)))
    return jax.tree.map(lambda _: found[next(numbers)], array)


def entering(array, axes, combine, identity, reverse):
    before = start = neutral_like(array, identity)
    running = array
    for axis in reversed(axes):
        size, index = (lax.axis_size(axis), lax.axis_index(axis))
        pieces = collected_together(running, axis)
        inside, running = (start, start)
        for k in reversed(range(size)) if reverse else range(size):
            passed = k > index if reverse else k < index
            running = combine(running, jax.tree.map(lambda part: part[k], pieces))
            inside = jax.tree.map(lambda new, old: jnp.where(passed, new, old), running, inside)
        before = combine(inside, before)
    return before


def from_partner(value, axis, distance):
    mask = 2**distance
    pairs = [(source, source ^ mask) for source in range(lax.axis_size(axis))]
    return lax.ppermute(value, axis, pairs)


def trig_tables(length):
    positions = jnp.arange(length, dtype=jnp.int32)
    product = positions[:, None] * positions[None, :] % length
    phase_angle = product.astype(jnp.float32) * (full_turn / length)
    return (jnp.cos(phase_angle), jnp.sin(phase_angle))


def multiply_by_unit_complex(values, phase_angle):
    cos_part = jnp.cos(phase_angle)
    sin_part = jnp.sin(phase_angle)
    real_part = values[:, 0] * cos_part - values[:, 1] * sin_part
    imag_part = values[:, 0] * sin_part + values[:, 1] * cos_part
    return jnp.stack([real_part, imag_part], axis=1)


def along_last(values, inverse):
    length = values.shape[-1]
    cos_table, sin_table = trig_tables(length)
    flattened = values.reshape(-1, length)
    with_cos = jnp.dot(
        flattened, cos_table, precision=exact_prec, preferred_element_type=jnp.float32
    ).reshape(values.shape)
    with_sin = jnp.dot(
        flattened, sin_table, precision=exact_prec, preferred_element_type=jnp.float32
    ).reshape(values.shape)
    if inverse:
        real_part = (with_cos[:, 0] - with_sin[:, 1]) / length
        imag_part = (with_cos[:, 1] + with_sin[:, 0]) / length
    else:
        real_part = with_cos[:, 0] + with_sin[:, 1]
        imag_part = with_cos[:, 1] - with_sin[:, 0]
    return jnp.stack([real_part, imag_part], axis=1)


def wave_squared(mode_ids, total_modes):
    signed_ids = jnp.where(mode_ids < total_modes // 2, mode_ids, mode_ids - total_modes).astype(
        jnp.float32
    )
    return (2.0 * signed_ids / total_modes) ** 2


def join_segments(left_seg, right_seg):
    z1f, z1l, v1f, v1l, w1f, w1l = left_seg
    z2f, z2l, v2f, v2l, w2f, w2l = right_seg
    divisor = 1.0 - w1l * v2f
    z_mid = (z1l - w1l * z2f) / divisor
    v_mid = v1l / divisor
    w_mid = -w1l * w2f / divisor
    z_next = z2f - v2f * z_mid
    v_next = -v2f * v_mid
    w_next = w2f - v2f * w_mid
    z_first = z1f - w1f * z_next
    v_first = v1f - w1f * v_next
    w_first = -w1f * w_next
    z_last = z2l - v2l * z_mid
    v_last = -v2l * v_mid
    w_last = w2l - v2l * w_mid
    return (z_first, z_last, v_first, v_last, w_first, w_last)


def join_reversed(earlier, later):
    return join_segments(later, earlier)


def thomas_sweep(lower_row, upper_row, kappa, rhs):
    row_count = rhs.shape[0]
    row_ids = jnp.arange(row_count, dtype=jnp.int32)
    left_rhs = jnp.where(row_ids == 0, lower_row, 0.0)
    right_rhs = jnp.where(row_ids == row_count - 1, upper_row, 0.0)
    zero_modes = jnp.zeros_like(kappa)

    def downward(carried, inputs):
        factor_prev, solved_prev, previous_left, right_prev = carried
        lower_here, upper_here, rhs_here, left_here, right_here = inputs
        divisor = -(lower_here + upper_here) - kappa - lower_here * factor_prev
        factor = upper_here / divisor
        solved = (rhs_here - lower_here * solved_prev) / divisor
        left_val = (left_here - lower_here * previous_left) / divisor
        right_val = (right_here - lower_here * right_prev) / divisor
        new_state = (factor, solved, left_val, right_val)
        return (new_state, new_state)

    start = (zero_modes, jnp.zeros_like(rhs[0]), zero_modes, zero_modes)
    _, stacked = lax.scan(downward, start, (lower_row, upper_row, rhs, left_rhs, right_rhs))

    def upward(carried, inputs):
        next_sol, next_left, next_right = carried
        factor, solved, left_val, right_val = inputs
        solution = solved - factor * next_sol
        left_sol = left_val - factor * next_left
        right_sol = right_val - factor * next_right
        new_state = (solution, left_sol, right_sol)
        return (new_state, new_state)

    _, results = lax.scan(
        upward, (jnp.zeros_like(rhs[0]), zero_modes, zero_modes), stacked, reverse=True
    )
    return results


def solve_modes(spectrum, kappa, lower_coef, upper_coef):
    row_count = spectrum.shape[0]
    chain_size = lax.axis_size(GY)
    my_row = lax.axis_index(GY)
    total_rows = row_count * chain_size
    row_ids = my_row * row_count + jnp.arange(row_count, dtype=jnp.int32)
    lower_eff = jnp.where(row_ids == 0, 0.0, lower_coef)
    upper_eff = jnp.where(row_ids == total_rows - 1, 0.0, upper_coef)
    inner, left_spike, right_spike = thomas_sweep(lower_eff, upper_eff, kappa, spectrum)
    own = (inner[0], inner[-1], left_spike[0], left_spike[-1], right_spike[0], right_spike[-1])
    zero_pair = jnp.zeros_like(inner[0])
    zero_modes = jnp.zeros_like(kappa)
    minus_one = -jnp.ones_like(kappa)
    identity = (zero_pair, zero_pair, zero_modes, minus_one, minus_one, zero_modes)
    below = entering(own, GY, join_segments, identity, False)
    above = entering(own, GY, join_reversed, identity, True)
    whole_above = join_segments(own, above)
    whole_below = join_segments(below, own)
    prev_last = (below[1] - below[5] * whole_above[0]) / (1.0 - below[5] * whole_above[2])
    next_first = (above[0] - above[2] * whole_below[1]) / (1.0 - above[2] * whole_below[5])
    return inner - left_spike[:, None] * prev_last[None] - right_spike[:, None] * next_first[None]


def local(source, lower_coef, upper_coef, span_wave):
    row_count, _, plane_count, local_streamwise = source.shape
    group_x = lax.axis_size("gx")
    my_x = lax.axis_index("gx")
    global_downstream_count = local_streamwise * group_x
    local_ids = jnp.arange(local_streamwise, dtype=jnp.int32)
    bit_count = group_x.bit_length() - 1
    spectrum = source
    for bit_number in range(bit_count - 1, -1, -1):
        partner = from_partner(spectrum, "gx", bit_number)
        upper_half = my_x // 2**bit_number % 2 == 1
        low_bits = my_x % 2**bit_number
        phase_angle = -(full_turn / 2 ** (bit_number + 1)) * low_bits.astype(jnp.float32)
        spectrum = jnp.where(
            upper_half,
            multiply_by_unit_complex(partner - spectrum, phase_angle),
            spectrum + partner,
        )
    reversed_index = jnp.zeros((), jnp.int32)
    for bit_number in range(bit_count):
        reversed_index = reversed_index + my_x // 2**bit_number % 2 * 2 ** (
            bit_count - 1 - bit_number
        )
    twiddle = -(full_turn / global_downstream_count) * (
        local_ids * reversed_index % global_downstream_count
    ).astype(jnp.float32)
    spectrum = along_last(multiply_by_unit_complex(spectrum, twiddle), False)
    mode_ids = reversed_index + group_x * local_ids
    kappa = span_wave[:, None] ** 2 + wave_squared(mode_ids, global_downstream_count)[None, :]
    solved = solve_modes(
        spectrum.reshape(row_count, 2, -1), kappa.reshape(-1), lower_coef, upper_coef
    )
    values = multiply_by_unit_complex(along_last(solved.reshape(source.shape), True), -twiddle)
    for bit_number in range(bit_count):
        partner = from_partner(values, "gx", bit_number)
        upper_half = my_x // 2**bit_number % 2 == 1
        low_bits = my_x % 2**bit_number
        phase_angle = full_turn / 2 ** (bit_number + 1) * low_bits.astype(jnp.float32)
        rotated = multiply_by_unit_complex(jnp.where(upper_half, values, partner), phase_angle)
        values = jnp.where(upper_half, partner - rotated, values + rotated) * 0.5
    return values


def solution(mesh):
    finer = Mesh(mesh.devices.reshape(mesh.shape["gx"], 8, 4), ("gx", "gy_0", "gy_1"))
    in_specs = (P(GY, None, None, "gx"), P(GY), P(GY), P())
    out_specs = P(GY, None, None, "gx")
    return jax.shard_map(local, mesh=finer, in_specs=in_specs, out_specs=out_specs, check_vma=False)
```

profile of v0, /device:TPU:1, one launch (start us, length us, event | category | flops | bytes accessed | tf_op | source)
XLA Modules:
  0.0 265.4 jit_solution(12474837598400823888)
XLA Ops:
  0.0 3.7 %collective-permute-start = (f32[16,2,8,256]{3,2,1,0:T(8,128)}, f32[16,2,8,256]{3,2,1,0:T(8,128)S(1)}, u32[]{:S(2)}, u32[]{:S(2)}) collective-permute-start(f32[16,2,8,256]{3,2,1,0:T(8,128)} %param.8), channel_id=1, source_target_pairs={{0,128},{32,160},{64,192},{96,224},{128,0},{160,32},{192,64},{224,... | collective-permute-start | bytes 786440 | tf_op jit(solution)/shard_map/ppermute | solution.py:57
  3.9 5.1 %collective-permute-done = f32[16,2,8,256]{3,2,1,0:T(8,128)S(1)} collective-permute-done((f32[16,2,8,256]{3,2,1,0:T(8,128)}, f32[16,2,8,256]{3,2,1,0:T(8,128)S(1)}, u32[]{:S(2)}, u32[]{:S(2)}) %collective-permute-start) | collective-permute-done | bytes 262176 | tf_op jit(solution)/shard_map/ppermute | solution.py:57
  9.0 1.0 sub.3999
  10.1 0.9 copy-done
  11.0 2.1 collective-permute-start.1
  13.4 4.4 %collective-permute-done.1 = f32[16,2,8,256]{3,2,1,0:T(8,128)S(1)} collective-permute-done((f32[16,2,8,256]{3,2,1,0:T(8,128)S(1)}, f32[16,2,8,256]{3,2,1,0:T(8,128)S(1)}, u32[]{:S(2)}, u32[]{:S(2)}) %collective-permute-start.1) | collective-permute-done | bytes 262176 | tf_op jit(solution)/shard_map/ppermute | solution.py:57
  17.9 2.7 %collective-permute-start.2 = (f32[16,2,8,256]{3,2,1,0:T(8,128)S(1)}, f32[16,2,8,256]{3,2,1,0:T(8,128)S(1)}, u32[]{:S(2)}, u32[]{:S(2)}) collective-permute-start(f32[16,2,8,256]{3,2,1,0:T(8,128)S(1)} %maximum_select_fusion.1), channel_id=1, source_target_pairs={{0,32},{32,0},{64,96},{96,64},{128,160},{160,128},{192,224},{224,1... | collective-permute-start | bytes 786440 | tf_op jit(solution)/shard_map/ppermute | solution.py:57
  22.3 1.4 fusion.19
  23.6 1.3 fusion.15
  25.7 136.8 %while.50 = (s32[]{:T(128)}, f32[2048]{0:T(1024)S(1)}, f32[2,2048]{1,0:T(2,128)S(1)}, f32[2048]{0:T(1024)S(1)}, f32[2048]{0:T(1024)S(1)}, /*index=5*/f32[16,2048...) while((s32[]{:T(128)}, f32[2048]{0:T(1024)S(1)}, ...), condition=%wide.region_1.2_spmd.clone, body=%wide.region_0.1_spmd.clone.sunk | while | flops 45061 | bytes 222537 | solution.py:143
  29.1 1.3 fusion.236
  31.0 1.9 fusion.237
  32.9 0.7 bitcast_dynamic-update-slice_fusion.4
  37.6 1.3 fusion.236
  39.6 1.9 fusion.237
  41.5 0.7 bitcast_dynamic-update-slice_fusion.4
  46.2 1.3 fusion.236
  48.1 1.9 fusion.237
  54.7 1.3 fusion.236
  56.7 1.9 fusion.237
  63.3 1.3 fusion.236
  65.2 1.9 fusion.237
  67.2 0.7 bitcast_dynamic-update-slice_fusion.4
  71.8 1.3 fusion.236
  73.8 1.9 fusion.237
  75.7 0.7 bitcast_dynamic-update-slice_fusion.4
  80.4 1.3 fusion.236
  82.3 1.9 fusion.237
  88.9 1.3 fusion.236
  90.9 1.9 fusion.237
  97.5 1.3 fusion.236
  99.4 1.9 fusion.237
  101.4 0.7 bitcast_dynamic-update-slice_fusion.4
  106.0 1.3 fusion.236
  108.0 1.9 fusion.237
  109.9 0.7 bitcast_dynamic-update-slice_fusion.4
  114.6 1.3 fusion.236
  116.5 1.9 fusion.237
  123.1 1.3 fusion.236
  125.1 1.9 fusion.237
  127.0 0.7 bitcast_dynamic-update-slice_fusion.4
  131.7 1.3 fusion.236
  133.6 1.9 fusion.237
  135.6 0.7 bitcast_dynamic-update-slice_fusion.4
  140.2 1.3 fusion.236
  142.2 1.9 fusion.237
  148.8 1.3 fusion.236
  150.7 1.9 fusion.237
  157.3 1.3 fusion.236
  159.3 1.9 fusion.237
  162.7 8.8 %while.51 = (s32[]{:T(128)}, f32[2,2048]{1,0:T(2,128)S(1)}, f32[2048]{0:T(1024)S(1)}, f32[2048]{0:T(1024)S(1)}, f32[16,2,2048]{2,1,0:T(2,128)S(1)}, /*index=5*/f...) while((s32[]{:T(128)}, f32[2,2048]{1,0:T(2,128)S(1)}, ...), condition=%wide.region_3.4_spmd.clone, body=%wide.region_2.3_spmd.clone.sunk | while | flops 24580 | bytes 213176 | solution.py:154
  171.6 10.1 %all-gather = f32[32,2048]{1,0:T(8,128)S(1)} all-gather(f32[8,2048]{1,0:T(8,128)S(1)} %concatenate.11), channel_id=2, replica_groups=mesh['gx'=8,'gy_0'=8,'gy_1'=4] {'gy_1'}, dimensions={0}, use_global_device_ids=true | all-gather | bytes 327680 | tf_op jit(solution)/shard_map/all_gather | solution.py:30
  182.9 22.9 %all-gather.2 = f32[64,2048]{1,0:T(8,128)S(1)} all-gather(f32[8,2048]{1,0:T(8,128)S(1)} %concatenate.13), channel_id=4, replica_groups=mesh['gx'=8,'gy_0'=8,'gy_1'=4] {'gy_0'}, dimensions={0}, use_global_device_ids=true | all-gather | bytes 589824 | tf_op jit(solution)/shard_map/all_gather | solution.py:30
  206.3 20.0 %all-gather.1 = f32[64,2048]{1,0:T(8,128)S(1)} all-gather(f32[8,2048]{1,0:T(8,128)S(1)} %concatenate.12), channel_id=3, replica_groups=mesh['gx'=8,'gy_0'=8,'gy_1'=4] {'gy_0'}, dimensions={0}, use_global_device_ids=true | all-gather | bytes 589824 | tf_op jit(solution)/shard_map/all_gather | solution.py:30
  228.3 1.2 divide_bitcast_fusion.1
  229.9 1.4 fusion.17
  231.3 1.3 fusion.13
  232.7 14.5 %collective-permute-start.3 = (f32[16,2,8,256]{3,2,1,0:T(8,128)S(1)}, f32[16,2,8,256]{3,2,1,0:T(8,128)S(1)}, u32[]{:S(2)}, u32[]{:S(2)}) collective-permute-start(f32[16,2,8,256]{3,2,1,0:T(8,128)S(1)} %pad_maximum_fusion.2), channel_id=1, source_target_pairs={{0,32},{32,0},{64,96},{96,64},{128,160},{160,128},{192,224},{224,1... | collective-permute-start | bytes 786440 | tf_op jit(solution)/shard_map/ppermute | solution.py:57
  247.3 1.2 collective-permute-done.3
  248.6 1.3 collective-permute-start.4
  250.1 6.1 %collective-permute-done.4 = f32[16,2,8,256]{3,2,1,0:T(8,128)S(1)} collective-permute-done((f32[16,2,8,256]{3,2,1,0:T(8,128)S(1)}, f32[16,2,8,256]{3,2,1,0:T(8,128)S(1)}, u32[]{:S(2)}, u32[]{:S(2)}) %collective-permute-start.4) | collective-permute-done | bytes 262176 | tf_op jit(solution)/shard_map/ppermute | solution.py:57
  256.4 3.0 %collective-permute-start.5 = (f32[16,2,8,256]{3,2,1,0:T(8,128)S(1)}, f32[16,2,8,256]{3,2,1,0:T(8,128)S(1)}, u32[]{:S(2)}, u32[]{:S(2)}) collective-permute-start(f32[16,2,8,256]{3,2,1,0:T(8,128)S(1)} %select_multiply_fusion.8), channel_id=1, source_target_pairs={{0,128},{32,160},{64,192},{96,224},{128,0},{160,32},{192,64},{224,... | collective-permute-start | bytes 786440 | tf_op jit(solution)/shard_map/ppermute | solution.py:57
  259.5 5.1 %collective-permute-done.5 = f32[16,2,8,256]{3,2,1,0:T(8,128)S(1)} collective-permute-done((f32[16,2,8,256]{3,2,1,0:T(8,128)S(1)}, f32[16,2,8,256]{3,2,1,0:T(8,128)S(1)}, u32[]{:S(2)}, u32[]{:S(2)}) %collective-permute-start.5) | collective-permute-done | bytes 262176 | tf_op jit(solution)/shard_map/ppermute | solution.py:57
  264.7 0.8 select_multiply_fusion.7
  (352 shorter events, 72.5 us)
Async XLA Ops:
  0.0 9.0 %collective-permute-start = (f32[16,2,8,256]{3,2,1,0:T(8,128)}, f32[16,2,8,256]{3,2,1,0:T(8,128)S(1)}, u32[]{:S(2)}, u32[]{:S(2)}) collective-permute-start(f32[16,2,8,256]{3,2,1,0:T(8,128)} %param.8), channel_id=1, source_target_pairs={{0,128},{32,160},{64,192},{96,224},{128,0},{160,32},{192,64},{224,... | collective-permute-start | bytes 786440 | tf_op jit(solution)/shard_map/ppermute | solution.py:57
  10.0 1.0 copy-start
  11.0 6.7 %collective-permute-start.1 = (f32[16,2,8,256]{3,2,1,0:T(8,128)S(1)}, f32[16,2,8,256]{3,2,1,0:T(8,128)S(1)}, u32[]{:S(2)}, u32[]{:S(2)}) collective-permute-start(f32[16,2,8,256]{3,2,1,0:T(8,128)S(1)} %maximum_select_fusion), channel_id=1, source_target_pairs={{0,64},{32,96},{64,0},{96,32},{128,192},{160,224},{192,128},{224,1... | collective-permute-start | bytes 786440 | tf_op jit(solution)/shard_map/ppermute | solution.py:57
  17.9 4.2 %collective-permute-start.2 = (f32[16,2,8,256]{3,2,1,0:T(8,128)S(1)}, f32[16,2,8,256]{3,2,1,0:T(8,128)S(1)}, u32[]{:S(2)}, u32[]{:S(2)}) collective-permute-start(f32[16,2,8,256]{3,2,1,0:T(8,128)S(1)} %maximum_select_fusion.1), channel_id=1, source_target_pairs={{0,32},{32,0},{64,96},{96,64},{128,160},{160,128},{192,224},{224,1... | collective-permute-start | bytes 786440 | tf_op jit(solution)/shard_map/ppermute | solution.py:57
  20.8 0.7 copy-start.3
  21.4 0.7 copy-start.1
  21.4 0.7 copy-start.2
  232.7 15.7 %collective-permute-start.3 = (f32[16,2,8,256]{3,2,1,0:T(8,128)S(1)}, f32[16,2,8,256]{3,2,1,0:T(8,128)S(1)}, u32[]{:S(2)}, u32[]{:S(2)}) collective-permute-start(f32[16,2,8,256]{3,2,1,0:T(8,128)S(1)} %pad_maximum_fusion.2), channel_id=1, source_target_pairs={{0,32},{32,0},{64,96},{96,64},{128,160},{160,128},{192,224},{224,1... | collective-permute-start | bytes 786440 | tf_op jit(solution)/shard_map/ppermute | solution.py:57
  248.6 7.6 %collective-permute-start.4 = (f32[16,2,8,256]{3,2,1,0:T(8,128)S(1)}, f32[16,2,8,256]{3,2,1,0:T(8,128)S(1)}, u32[]{:S(2)}, u32[]{:S(2)}) collective-permute-start(f32[16,2,8,256]{3,2,1,0:T(8,128)S(1)} %select_multiply_fusion.9), channel_id=1, source_target_pairs={{0,64},{32,96},{64,0},{96,32},{128,192},{160,224},{192,128},{224,1... | collective-permute-start | bytes 786440 | tf_op jit(solution)/shard_map/ppermute | solution.py:57
  256.4 8.2 %collective-permute-start.5 = (f32[16,2,8,256]{3,2,1,0:T(8,128)S(1)}, f32[16,2,8,256]{3,2,1,0:T(8,128)S(1)}, u32[]{:S(2)}, u32[]{:S(2)}) collective-permute-start(f32[16,2,8,256]{3,2,1,0:T(8,128)S(1)} %select_multiply_fusion.8), channel_id=1, source_target_pairs={{0,128},{32,160},{64,192},{96,224},{128,0},{160,32},{192,64},{224,... | collective-permute-start | bytes 786440 | tf_op jit(solution)/shard_map/ppermute | solution.py:57
where the time goes:
time: 267 us; the launch traced here: 265 us
  other arithmetic  72.2 us (27%)
  local copies, waits for them, and re-layouts  61.4 us (23%)
  blocking collectives  53 us (20%)
  starting transfers between devices  27.3 us (10%)
  loops' own time  22.9 us (9%)
  waiting for transfers between devices  21.9 us (8%)
  matrix products  5.41 us (2%)
    all_gather x3, blocking collectives, collected_together(): both, at, found = (lax.all_gather(jnp.concatenate(lines), axis), 0, {})  53 us
    dynamic_slice x64, local copies, waits for them, and re-layouts, thomas_sweep(): lax.scan(downward, start, (lower_row, upper_row, rhs, left_rhs, right_rhs))  40.9 us
    div x16, other arithmetic, downward(): left_val = (left_here - lower_here * previous_left) / divisor  30.9 us
    ppermute x6, starting transfers between devices, from_partner(): return lax.ppermute(value, axis, pairs)  27.3 us
    another operation x1, loops' own time, thomas_sweep(): lax.scan(downward, start, (lower_row, upper_row, rhs, left_rhs, right_rhs))  22 us
    ppermute x6, waiting for transfers between devices, from_partner(): return lax.ppermute(value, axis, pairs)  21.9 us
    div x16, other arithmetic, downward(): right_val = (right_here - lower_here * right_prev) / divisor  20.8 us
    dynamic_update_slice x80, local copies, waits for them, and re-layouts, thomas_sweep(): lax.scan(downward, start, (lower_row, upper_row, rhs, left_rhs, right_rhs))  16.4 us
  transfers between devices with their start and end apart: 6, of which 5 were waited for; matrix products, arithmetic and copies ran while one was open for 0% of the time, Pallas kernels for 0%

commit v1 on v0

v1 whole, which is shorter than its diff:
```python
import functools
import math

import jax
import jax.numpy as jnp
import numpy as np
from jax import lax
from jax.experimental import pallas as pl
from jax.experimental.pallas import tpu as pltpu
from jax.sharding import PartitionSpec as P

MESH = pl.DeviceIdType.MESH
HIGHEST = lax.Precision.HIGHEST

ROWS = 16
PLANES = 8
NX = 2048
LANES = 128
RADIX = 16
NZ = 8
NXP = 4
BLOCKS = NZ * NXP


def transform_constants():
    lanes = np.arange(LANES)
    angle = 2.0 * np.pi * (np.outer(lanes, lanes) % LANES) / LANES
    c, s = np.cos(angle), np.sin(angle)
    matrix = np.block([[c, -s], [s, c]]).astype(np.float32)
    twist = 2.0 * np.pi * (np.outer(np.arange(RADIX), lanes) % NX) / NX
    twiddle = np.concatenate([np.cos(twist), np.sin(twist)]).astype(np.float32)
    return matrix, twiddle


def rotated(value, index, size, inverse):
    re, im = value
    index = index % size
    if index == 0:
        return value
    if 4 * index == size:
        return (-im, re) if inverse else (im, -re)
    c = math.cos(2.0 * math.pi * index / size)
    s = math.sin(2.0 * math.pi * index / size)
    if not inverse:
        s = -s
    return (re * c - im * s, re * s + im * c)


def butterflies(values, inverse):
    size = len(values)
    if size == 1:
        return values
    even = butterflies(values[0::2], inverse)
    odd = butterflies(values[1::2], inverse)
    odd = [rotated(o, k, size, inverse) for k, o in enumerate(odd)]
    low = [(e[0] + o[0], e[1] + o[1]) for e, o in zip(even, odd)]
    high = [(e[0] - o[0], e[1] - o[1]) for e, o in zip(even, odd)]
    return low + high


def kernel(
    source, lower_hbm, upper_hbm, span_hbm, matrix_hbm, twiddle_hbm, fbuf,
    src, sbuf, rbuf, ure, uim, spec, matrix, twiddle, lower, upper, span,
    coef, mbuf, abuf, wbuf, gbuf, gin, alone, factors,
    raw, gz, zrecv, obuf,
    load_sem, fs_sem, fr_sem, cxs_sem, cxr_sem, czs_sem, czr_sem,
    zs_sem, zr_sem, xs_sem, xr_sem, bs_sem, br_sem, near_sem, far_sem,
):
    gx = lax.axis_index("gx")
    gy = lax.axis_index("gy")
    zi = gy // NXP
    xi = gy % NXP
    base = zi * NXP

    chip, core = gx // 2, gx % 2
    gx_peers = [lax.rem(chip + d, PLANES // 2) * 2 + lax.rem(core + c, 2)
                for d, c in ((2, 0), (2, 1), (1, 0), (3, 0), (1, 1), (3, 1), (0, 1))]
    x_peers = [lax.rem(xi + d, NXP) for d in (2, 1, 3)]
    z_peers = [lax.rem(zi + d, NZ) for d in (4, 3, 5, 2, 6, 1, 7)]

    def at_gx(q):
        return (q, gy)

    def at_x(q):
        return (gx, base + q)

    def at_z(q):
        return (gx, q * NXP + xi)

    z_near = [lax.rem(zi + d, NZ) for d in (1, NZ - 1)]
    z_far = [lax.rem(zi + d, NZ) for d in (2, NZ - 2)]
    near = [at_z(q) for q in z_near] + [at_x(q) for q in x_peers] + [at_gx(q) for q in gx_peers]
    barrier = pltpu.get_barrier_semaphore()
    for device in near:
        pl.semaphore_signal(barrier, inc=1, device_id=device, device_id_type=MESH)

    loads = []
    for part in range(2):
        for xt in range(2):
            loads.append(pltpu.make_async_copy(
                source.at[:, part, :, pl.ds(xt * LANES, LANES)], src.at[xt, part],
                load_sem.at[2 * xt + part]))
    for n, (there, here) in enumerate(((lower_hbm, lower), (upper_hbm, upper), (span_hbm, span),
                                       (matrix_hbm, matrix), (twiddle_hbm, twiddle))):
        loads.append(pltpu.make_async_copy(there, here, load_sem.at[4 + n]))
    for load in loads:
        load.start()

    for load in loads[:4]:
        load.wait()
    flat = src.reshape(4 * ROWS * PLANES, LANES)
    for q in range(PLANES):
        sbuf[q] = flat[pl.ds(q, 4 * ROWS, stride=PLANES), :]
    rbuf[gx] = sbuf[gx]

    for load in loads[4:]:
        load.wait()
    first, last = gy == 0, gy == BLOCKS - 1
    low = [lower[i] for i in range(ROWS)]
    upp = [upper[i] for i in range(ROWS)]
    low[0] = jnp.where(first, 0.0, low[0])
    upp[-1] = jnp.where(last, 0.0, upp[-1])
    sums, lost = [], []
    for l, u in zip(low, upp):
        total = l + u
        rest = total - l
        sums.append(total)
        lost.append(-((l - (total - rest)) + (u - rest)))
    lane = lax.broadcasted_iota(jnp.int32, (1, LANES), 1)
    row = jnp.zeros((1, LANES), jnp.float32)
    for i, value in enumerate(low + upp + sums + lost + upp[::-1] + low[::-1] + sums[::-1] + lost[::-1]):
        row = jnp.where(lane == i, value, row)
    coef[gy] = row

    pl.semaphore_wait(barrier, len(near))

    def remote(src_ref, dst_ref, send, recv, device):
        return pltpu.make_async_remote_copy(
            src_ref=src_ref, dst_ref=dst_ref, send_sem=send, recv_sem=recv,
            device_id=device, device_id_type=MESH)

    forward = [remote(sbuf.at[q], rbuf.at[gx], fs_sem.at[q], fr_sem.at[gx], at_gx(q)) for q in gx_peers]
    coef_x = [remote(coef.at[gy], coef.at[gy], cxs_sem.at[q], cxr_sem.at[xi], at_x(q)) for q in x_peers]
    for copy in coef_x + forward:
        copy.start()
    for q in z_near:
        pl.semaphore_signal(near_sem, inc=1, device_id=at_z(q), device_id_type=MESH)

    k1 = lax.broadcasted_iota(jnp.int32, (RADIX, LANES), 0)
    k2 = lax.broadcasted_iota(jnp.int32, (RADIX, LANES), 1)
    mode = k1 + RADIX * k2
    signed = jnp.where(mode < NX // 2, mode, mode - NX).astype(jnp.float32)
    wave = 2.0 * signed / NX
    kappa = span[gx] * span[gx] + wave * wave
    one = jnp.ones((RADIX, LANES), jnp.float32)

    def pivots(order, ahead, behind, g, keep, into):
        for i in order:
            l, u = ahead[i], behind[i]
            s = (((sums[i] + kappa) - sums[i]) + lost[i]) + l * g
            inv = 1.0 / (u + s)
            g = s * inv
            keep[into, i] = l * inv
            keep[into + 1, i] = inv
            if keep is factors:
                keep[into + 2, i] = u * inv
        return g

    pivots(range(ROWS), low, upp, one, alone, 0)
    pivots(range(ROWS - 1, -1, -1), upp, low, one, alone, 2)

    pl.semaphore_wait(near_sem, 2)
    for q in z_far:
        pl.semaphore_signal(far_sem, inc=1, device_id=at_z(q), device_id_type=MESH)

    for q in x_peers:
        there = coef.at[base + q]
        remote(there, there, cxs_sem.at[q], cxr_sem.at[q], at_x(q)).wait_recv()
    pl.semaphore_wait(far_sem, 2)
    group = coef.at[pl.ds(base, NXP)]
    coef_z = [remote(group, group, czs_sem.at[q], czr_sem.at[zi], at_z(q)) for q in z_peers]
    for copy in coef_z:
        copy.start()

    def block_product(t, way):
        row = jnp.broadcast_to(coef[t], (8, LANES))
        turned = pltpu.roll(row, LANES // 2, 1)
        row = jnp.where(way == 0, row, turned)

        def splat(i):
            one = jnp.broadcast_to(row[:, i : i + 1], (8, LANES))
            return one, jnp.concatenate([one, one], axis=0)

        scale = None
        for i in range(ROWS):
            one, l = splat(i)
            _, u = splat(ROWS + i)
            _, total = splat(2 * ROWS + i)
            _, gained = splat(3 * ROWS + i)
            rounded = ((total + kappa) - total) + gained
            if i == 0:
                scale, a, b, c, d = one, l, rounded, l, u + rounded
                continue
            scale = scale * one
            a = l * a + rounded * c
            b = l * b + rounded * d
            c = a + u * c
            d = b + u * d
        mbuf[way, t, 0] = a
        mbuf[way, t, 1] = b
        mbuf[way, t, 2] = c
        mbuf[way, t, 3] = d
        mbuf[way, t, 4] = jnp.concatenate([scale, scale], axis=0)

    @pl.loop(0, 2)
    def _(way):
        for j in range(NXP):
            block_product(base + j, way)

    for q in gx_peers:
        remote(sbuf.at[q], rbuf.at[q], fs_sem.at[q], fr_sem.at[q], at_gx(q)).wait_recv()
    values = []
    for a in range(RADIX):
        at = (a % 2) * 32
        values.append((rbuf[a // 2, at : at + ROWS, :], rbuf[a // 2, at + ROWS : at + 2 * ROWS, :]))
    values = butterflies(values, False)
    for k in range(RADIX):
        re, im = values[k]
        c, s = twiddle[k : k + 1, :], twiddle[RADIX + k : RADIX + k + 1, :]
        ure[pl.ds(k, ROWS, stride=RADIX), :] = re * c + im * s
        uim[pl.ds(k, ROWS, stride=RADIX), :] = im * c - re * s
    both = jnp.concatenate([ure[...], uim[...]], axis=1)
    spec[...] = jnp.dot(both, matrix[...], precision=HIGHEST, preferred_element_type=jnp.float32)

    def rhs(i, part):
        return spec[i * RADIX : (i + 1) * RADIX, part * LANES : (part + 1) * LANES]

    for way, order in enumerate((range(ROWS), range(ROWS - 1, -1, -1))):
        for part in range(2):
            y = None
            for i in order:
                r = rhs(i, part) * alone[2 * way + 1, i]
                y = -r if y is None else alone[2 * way, i] * y - r
            raw[xi, (2 * way + part) * RADIX : (2 * way + part + 1) * RADIX, :] = y
    to_x = [remote(raw.at[xi], raw.at[xi], xs_sem.at[q], xr_sem.at[xi], at_x(q)) for q in x_peers]
    for copy in to_x:
        copy.start()

    @pl.loop(0, NZ - 1)
    def _(n):
        step = n // 2 + 1
        q = lax.rem(zi + jnp.where(n % 2 == 0, step, NZ - step), NZ)
        there = coef.at[pl.ds(q * NXP, NXP)]
        remote(there, there, czs_sem.at[q], czr_sem.at[q], at_z(q)).wait_recv()
        for j in range(NXP):
            block_product(q * NXP + j, (q > zi).astype(jnp.int32))

    gbuf[...] = jnp.zeros_like(gbuf)

    def advance(t, way):
        g = gbuf[way]
        inv = 1.0 / (mbuf[way, t, 2] * g + mbuf[way, t, 3])
        gbuf[way] = (mbuf[way, t, 0] * g + mbuf[way, t, 1]) * inv
        abuf[way, t] = mbuf[way, t, 4] * inv
        return g

    @pl.loop(0, BLOCKS - NXP)
    def _(n):
        above = (n >= base).astype(jnp.int32)
        advance(jnp.where(n < base, n, BLOCKS - 1 - (n - base)), above)

    for j in range(NXP):
        gin[0, j] = advance(base + j, 0)
        gin[1, NXP - 1 - j] = advance(base + NXP - 1 - j, 1)

    for q in x_peers:
        remote(raw.at[q], raw.at[q], xs_sem.at[q], xr_sem.at[q], at_x(q)).wait_recv()
    entering = []
    for way, order in enumerate((range(NXP), range(NXP - 1, -1, -1))):
        run, mine = [jnp.zeros_like(one)] * 2, [jnp.zeros_like(one)] * 2
        for j in order:
            here = xi == j
            a = abuf[way, base + j]
            ae = a * (1.0 - gin[way, j])
            for part in range(2):
                end = raw[j, (2 * way + part) * RADIX : (2 * way + part + 1) * RADIX, :]
                start = raw[j, (2 - 2 * way + part) * RADIX : (3 - 2 * way + part) * RADIX, :]
                mine[part] = jnp.where(here, run[part], mine[part])
                run[part] = a * run[part] + (end + ae * start)
        for part in range(2):
            gz[way, part * RADIX : (part + 1) * RADIX, :] = run[part]
        entering.append(mine)

    to_z = []
    for q in z_peers:
        which = jnp.where(q > zi, 0, 1)
        to_z.append(remote(gz.at[which], zrecv.at[zi], zs_sem.at[q], zr_sem.at[zi], at_z(q)))
    for copy in to_z:
        copy.start()

    def down(n, run):
        t = gy - 1 - n
        wbuf[t] = run
        return run * abuf[0, t]

    def below(n, run):
        t = base - 1 - n
        wbuf[t] = run
        return run * abuf[0, t]

    pre = lax.fori_loop(0, xi, down, one)
    lax.fori_loop(0, base, below, one)

    def up(n, run):
        return run * abuf[1, gy + 1 + n]

    def above(n, run):
        t = base + NXP + n
        wbuf[t] = run
        return run * abuf[1, t]

    post = lax.fori_loop(0, NXP - 1 - xi, up, one)
    lax.fori_loop(0, BLOCKS - NXP - base, above, one)

    g_end = pivots(range(ROWS), low, upp, gin[0, xi], factors, 0)
    h_in = gin[1, xi]
    scale = 1.0 / (g_end + h_in * factors[2, ROWS - 1])

    sy = [jnp.zeros_like(one)] * 2
    sz = [jnp.zeros_like(one)] * 2
    for q in z_peers[::-1]:
        remote(gz.at[0], zrecv.at[q], zs_sem.at[q], zr_sem.at[q], at_z(q)).wait_recv()
        lower_side = q < zi
        w = wbuf[q * NXP + jnp.where(lower_side, NXP - 1, 0)]
        wy = jnp.where(lower_side, w, 0.0)
        wz = jnp.where(lower_side, 0.0, w)
        for part in range(2):
            v = zrecv[q, part * RADIX : (part + 1) * RADIX, :]
            sy[part] = sy[part] + wy * v
            sz[part] = sz[part] + wz * v

    ends = [[], []]
    for part in range(2):
        y = entering[0][part] + pre * sy[part]
        for i in range(ROWS):
            y = factors[0, i] * y - factors[1, i] * rhs(i, part)
            ends[part].append(y)
    for part in range(2):
        ref = uim if part else ure
        z_in = entering[1][part] + post * sz[part]
        x = (factors[2, ROWS - 1] * z_in + ends[part][-1]) * scale
        for i in range(ROWS - 1, -1, -1):
            if i < ROWS - 1:
                x = factors[2, i] * x + ends[part][i]
            ref[i * RADIX : (i + 1) * RADIX, :] = x

    both = jnp.concatenate([ure[...], uim[...]], axis=1)
    back = lax.dot_general(both, matrix[...], (((1,), (1,)), ((), ())), precision=HIGHEST,
                           preferred_element_type=jnp.float32)
    ure[...] = back[:, :LANES]
    uim[...] = back[:, LANES:]
    values = []
    for k in range(RADIX):
        re = ure[pl.ds(k, ROWS, stride=RADIX), :]
        im = uim[pl.ds(k, ROWS, stride=RADIX), :]
        c = twiddle[k : k + 1, :] * (1.0 / NX)
        s = twiddle[RADIX + k : RADIX + k + 1, :] * (1.0 / NX)
        values.append((re * c - im * s, im * c + re * s))
    values = butterflies(values, True)
    for a in range(RADIX):
        at = (a % 2) * 32
        obuf[a // 2, at : at + ROWS, :] = values[a][0]
        obuf[a // 2, at + ROWS : at + 2 * ROWS, :] = values[a][1]
    backward = [remote(obuf.at[q], fbuf.at[gx], bs_sem.at[q], br_sem.at[gx], at_gx(q)) for q in gx_peers]
    for copy in backward:
        copy.start()
    own = pltpu.make_async_copy(obuf.at[gx], fbuf.at[gx], load_sem.at[0])
    own.start()
    for copy in coef_x + forward + coef_z + to_z + to_x:
        copy.wait_send()
    own.wait()
    for q in gx_peers:
        remote(obuf.at[q], fbuf.at[q], bs_sem.at[q], br_sem.at[q], at_gx(q)).wait_recv()
    for copy in backward:
        copy.wait_send()


def assemble(fbuf, out):
    for q in range(PLANES):
        for xt in range(2):
            for part in range(2):
                at = (xt * 2 + part) * ROWS
                out[pl.ds((part * 2 + xt) * PLANES + q, ROWS, stride=4 * PLANES), :] = fbuf[q, at : at + ROWS, :]


def local(source, lower, upper, span):
    matrix, twiddle = transform_constants()
    f32 = jnp.float32
    dma = pltpu.SemaphoreType.DMA
    vmem = lambda *shape: pltpu.VMEM(shape, f32)
    smem = lambda *shape: pltpu.SMEM(shape, f32)
    any_spec = pl.BlockSpec(memory_space=pl.ANY)
    planes = pl.pallas_call(
        kernel,
        out_shape=jax.ShapeDtypeStruct((PLANES, 64, LANES), f32),
        in_specs=[pl.BlockSpec(memory_space=pltpu.HBM)] * 6,
        out_specs=any_spec,
        scratch_shapes=[
            vmem(2, 2, ROWS, PLANES, LANES), vmem(PLANES, 64, LANES), vmem(PLANES, 64, LANES),
            vmem(256, LANES), vmem(256, LANES), vmem(256, 256), vmem(256, 256), vmem(2 * RADIX, LANES),
            smem(ROWS), smem(ROWS), smem(PLANES),
            vmem(BLOCKS, 1, LANES), vmem(2, BLOCKS, 5, RADIX, LANES), vmem(2, BLOCKS, RADIX, LANES),
            vmem(BLOCKS, RADIX, LANES), vmem(2, RADIX, LANES), vmem(2, NXP, RADIX, LANES),
            vmem(4, ROWS, RADIX, LANES), vmem(3, ROWS, RADIX, LANES),
            vmem(NXP, 64, LANES), vmem(2, 32, LANES), vmem(NZ, 32, LANES), vmem(PLANES, 64, LANES),
            dma((9,)), dma((PLANES,)), dma((PLANES,)), dma((NXP,)), dma((NXP,)), dma((NZ,)), dma((NZ,)),
            dma((NZ,)), dma((NZ,)), dma((NXP,)), dma((NXP,)), dma((PLANES,)), dma((PLANES,)),
            pltpu.SemaphoreType.REGULAR, pltpu.SemaphoreType.REGULAR,
        ],
        compiler_params=pltpu.CompilerParams(
            collective_id=0, has_side_effects=True, vmem_limit_bytes=16 * 1024 * 1024),
    )(*[pltpu.with_memory_space_constraint(x, pltpu.HBM)
        for x in (source, lower, upper, span, jnp.asarray(matrix), jnp.asarray(twiddle))])
    result = pl.pallas_call(
        assemble,
        out_shape=jax.ShapeDtypeStruct((ROWS * 4 * PLANES, LANES), f32),
        in_specs=[pl.BlockSpec(memory_space=pltpu.VMEM)],
        out_specs=pl.BlockSpec(memory_space=pltpu.VMEM),
        compiler_params=pltpu.CompilerParams(vmem_limit_bytes=4 * 1024 * 1024),
    )(planes)
    result = result.reshape(ROWS, 2, 2, PLANES, LANES)
    return result.transpose(0, 1, 3, 2, 4).reshape(source.shape)


def solution(mesh):
    in_specs = (P("gy", None, None, "gx"), P("gy"), P("gy"), P())
    out_specs = P("gy", None, None, "gx")
    return jax.shard_map(local, mesh=mesh, in_specs=in_specs, out_specs=out_specs, check_vma=False)
```

time: 267 us -> 32.6 us (0.12)
  other arithmetic: 72.2 us -> 0 us
  local copies, waits for them, and re-layouts: 61.4 us -> 0 us
  blocking collectives: 53 us -> 0 us
  Pallas kernels: 0 us -> 32.5 us
  starting transfers between devices: 27.3 us -> 0 us
  loops' own time: 22.9 us -> 0 us
  waiting for transfers between devices: 21.9 us -> 0 us
  matrix products: 5.41 us -> 0 us
    all_gather x3 -> x0, blocking collectives: 53 us -> none  [collected_together(): both, at, found = (lax.all_gather(jnp.concatenate(lines), axis), 0, {})]
    div x32 -> x0, other arithmetic: 51.7 us -> none  [the longest x16 30.9 us: downward(): left_val = (left_here - lower_here * previous_left) / divisor]
    dynamic_slice x96 -> x0, local copies, waits for them, and re-layouts: 41.4 us -> none  [the longest x64 40.9 us: thomas_sweep(): lax.scan(downward, start, (lower_row, upper_row, rhs, left_rhs, right_rhs))]
    pallas_call x0 -> x2, Pallas kernels: none -> 32.5 us  [the longest x1 31.6 us: local(): pl.pallas_call(kernel, out_shape=jax.ShapeDtypeStruct((PLANES, 64, LANES)...]
    ppermute x6 -> x0, starting transfers between devices: 27.3 us -> none  [from_partner(): return lax.ppermute(value, axis, pairs)]
    another operation x2 -> x0, loops' own time: 22.9 us -> none  [the longest x1 22 us: thomas_sweep(): lax.scan(downward, start, (lower_row, upper_row, rhs, left_rhs, right_rhs))]
    ppermute x6 -> x0, waiting for transfers between devices: 21.9 us -> none  [from_partner(): return lax.ppermute(value, axis, pairs)]
    dynamic_update_slice x80 -> x0, local copies, waits for them, and re-layouts: 16.4 us -> none  [thomas_sweep(): lax.scan(downward, start, (lower_row, upper_row, rhs, left_rhs, right_rhs))]
  transfers between devices with their start and end apart: 6 -> 0, of which waited for: 5 -> 0; matrix products, arithmetic and copies ran while one was open for 0% -> 0% of each run, Pallas kernels for 0% -> 0%
where the time goes in v1:
time: 32.6 us; the launch traced here: 32.5 us
  Pallas kernels  32.5 us (100%)
    pallas_call x1, Pallas kernels, local(): pl.pallas_call(kernel, out_shape=jax.ShapeDtypeStruct((PLANES, 64, LANES)...  31.6 us
    pallas_call x1, Pallas kernels, local(): pl.pallas_call(assemble, out_shape=jax.ShapeDtypeStruct((ROWS * 4 * PLANE...  0.91 us

profile of v1, /device:TPU:1, one launch (start us, length us, event | category | flops | bytes accessed | tf_op | source)
XLA Modules:
  0.0 32.5 jit_solution(16509184779060559854)
XLA Ops:
  0.0 31.6 %shard_map.64.fbuf = f32[8,64,128]{2,1,0:T(8,128)S(1)} custom-call(f32[16,2,8,256]{3,2,1,0:T(8,128)} %source.1, f32[16]{0:T(128)} %lower_hbm.1, f32[16]{0:T(128)} %upper_hbm.1, f32[8]{0:T(128)} %span_hbm.1, f32[256,256]{1,0:T(8,128)} %constant.4.clone.matrix_hbm, f32[32,128]{1,0:T(8,128)} %constant.5.clone.twiddle_hbm), custom_call_target="tpu_custom_call" | custom-call | tf_op jit(solution)/shard_map/pallas_call | solution.py:403
  31.6 0.9 %shard_map.65 = f32[512,128]{1,0:T(8,128)} custom-call(f32[8,64,128]{2,1,0:T(8,128)S(1)} %shard_map.64.fbuf), custom_call_target="tpu_custom_call" | custom-call | tf_op jit(solution)/shard_map/pallas_call | solution.py:424

commit v2 on v1

--- a/solution.py
+++ b/solution.py
@@ -1,8 +1,8 @@
-import functools
 import math
 
 import jax
 import jax.numpy as jnp
+import ml_dtypes
 import numpy as np
 from jax import lax
 from jax.experimental import pallas as pl
@@ -10,7 +10,6 @@
 from jax.sharding import PartitionSpec as P
 
 MESH = pl.DeviceIdType.MESH
-HIGHEST = lax.Precision.HIGHEST
 
 ROWS = 16
 PLANES = 8
@@ -27,6 +26,11 @@
     angle = 2.0 * np.pi * (np.outer(lanes, lanes) % LANES) / LANES
     c, s = np.cos(angle), np.sin(angle)
     matrix = np.block([[c, -s], [s, c]]).astype(np.float32)
+    terms, rest = [], matrix
+    for _ in range(3):
+        terms.append(rest.astype(ml_dtypes.bfloat16))
+        rest = rest - terms[-1].astype(np.float32)
+    matrix = np.concatenate([terms[0], terms[1], terms[2], terms[0], terms[1], terms[0]])
     twist = 2.0 * np.pi * (np.outer(np.arange(RADIX), lanes) % NX) / NX
     twiddle = np.concatenate([np.cos(twist), np.sin(twist)]).astype(np.float32)
     return matrix, twiddle
@@ -58,13 +62,32 @@
     return low + high
 
 
+def product(x, matrix):
+    high = x.astype(jnp.bfloat16)
+    rest = x - high.astype(jnp.float32)
+    middle = rest.astype(jnp.bfloat16)
+    low = (rest - middle.astype(jnp.float32)).astype(jnp.bfloat16)
+    terms = jnp.concatenate([high, high, high, middle, middle, low], axis=1)
+    return jnp.dot(terms, matrix, preferred_element_type=jnp.float32)
+
+
+def times(x, y):
+    a, b, c, d = x
+    e, f, g, h = y
+    return (a * e + b * g, a * f + b * h, c * e + d * g, c * f + d * h)
+
+
+def scaled(x):
+    r = pl.reciprocal(x[2] + x[3], approx=True)
+    return tuple(v * r for v in x)
+
+
 def kernel(
     source, lower_hbm, upper_hbm, span_hbm, matrix_hbm, twiddle_hbm, fbuf,
     src, sbuf, rbuf, ure, uim, spec, matrix, twiddle, lower, upper, span,
-    coef, mbuf, abuf, wbuf, gbuf, gin, alone, factors,
+    coef, mbuf, abuf, wbuf, gbuf, gin, chain, alone, factors,
     raw, gz, zrecv, obuf,
-    load_sem, fs_sem, fr_sem, cxs_sem, cxr_sem, czs_sem, czr_sem,
-    zs_sem, zr_sem, xs_sem, xr_sem, bs_sem, br_sem, near_sem, far_sem,
+    load_sem, send_sem, recv_sem, cxr_sem, czr_sem, near_sem, far_sem,
 ):
     gx = lax.axis_index("gx")
     gy = lax.axis_index("gy")
@@ -90,30 +113,38 @@
     z_near = [lax.rem(zi + d, NZ) for d in (1, NZ - 1)]
     z_far = [lax.rem(zi + d, NZ) for d in (2, NZ - 2)]
     near = [at_z(q) for q in z_near] + [at_x(q) for q in x_peers] + [at_gx(q) for q in gx_peers]
+    loads = [pltpu.make_async_copy(there, here, load_sem.at[n]) for n, (there, here) in enumerate((
+        (source, src), (lower_hbm, lower), (upper_hbm, upper), (span_hbm, span),
+        (twiddle_hbm, twiddle), (matrix_hbm, matrix)))]
+    loads[0].start()
     barrier = pltpu.get_barrier_semaphore()
     for device in near:
         pl.semaphore_signal(barrier, inc=1, device_id=device, device_id_type=MESH)
-
-    loads = []
-    for part in range(2):
+    for load in loads[1:]:
+        load.start()
+
+    loads[0].wait()
+    for q in range(PLANES):
         for xt in range(2):
-            loads.append(pltpu.make_async_copy(
-                source.at[:, part, :, pl.ds(xt * LANES, LANES)], src.at[xt, part],
-                load_sem.at[2 * xt + part]))
-    for n, (there, here) in enumerate(((lower_hbm, lower), (upper_hbm, upper), (span_hbm, span),
-                                       (matrix_hbm, matrix), (twiddle_hbm, twiddle))):
-        loads.append(pltpu.make_async_copy(there, here, load_sem.at[4 + n]))
-    for load in loads:
-        load.start()
-
-    for load in loads[:4]:
-        load.wait()
-    flat = src.reshape(4 * ROWS * PLANES, LANES)
-    for q in range(PLANES):
-        sbuf[q] = flat[pl.ds(q, 4 * ROWS, stride=PLANES), :]
+            for part in range(2):
+                at = (xt * 2 + part) * ROWS
+                sbuf[q, at : at + ROWS, :] = src[pl.ds((part * 2 + xt) * PLANES + q, ROWS, stride=4 * PLANES), :]
+
+    pl.semaphore_wait(barrier, len(near))
+
+    def remote(src_ref, dst_ref, send, recv, device):
+        return pltpu.make_async_remote_copy(
+            src_ref=src_ref, dst_ref=dst_ref, send_sem=send, recv_sem=recv,
+            device_id=device, device_id_type=MESH)
+
+    forward = [remote(sbuf.at[q], rbuf.at[gx], send_sem.at[0], recv_sem.at[0], at_gx(q)) for q in gx_peers]
+    for copy in forward:
+        copy.start()
+    for q in z_near:
+        pl.semaphore_signal(near_sem, inc=1, device_id=at_z(q), device_id_type=MESH)
     rbuf[gx] = sbuf[gx]
 
-    for load in loads[4:]:
+    for load in loads[1:4]:
         load.wait()
     first, last = gy == 0, gy == BLOCKS - 1
     low = [lower[i] for i in range(ROWS)]
@@ -132,19 +163,9 @@
         row = jnp.where(lane == i, value, row)
     coef[gy] = row
 
-    pl.semaphore_wait(barrier, len(near))
-
-    def remote(src_ref, dst_ref, send, recv, device):
-        return pltpu.make_async_remote_copy(
-            src_ref=src_ref, dst_ref=dst_ref, send_sem=send, recv_sem=recv,
-            device_id=device, device_id_type=MESH)
-
-    forward = [remote(sbuf.at[q], rbuf.at[gx], fs_sem.at[q], fr_sem.at[gx], at_gx(q)) for q in gx_peers]
-    coef_x = [remote(coef.at[gy], coef.at[gy], cxs_sem.at[q], cxr_sem.at[xi], at_x(q)) for q in x_peers]
-    for copy in coef_x + forward:
-        copy.start()
-    for q in z_near:
-        pl.semaphore_signal(near_sem, inc=1, device_id=at_z(q), device_id_type=MESH)
+    coef_x = [remote(coef.at[gy], coef.at[gy], send_sem.at[1], cxr_sem.at[xi], at_x(q)) for q in x_peers]
+    for copy in coef_x:
+        copy.start()
 
     k1 = lax.broadcasted_iota(jnp.int32, (RADIX, LANES), 0)
     k2 = lax.broadcasted_iota(jnp.int32, (RADIX, LANES), 1)
@@ -175,10 +196,10 @@
 
     for q in x_peers:
         there = coef.at[base + q]
-        remote(there, there, cxs_sem.at[q], cxr_sem.at[q], at_x(q)).wait_recv()
+        remote(there, there, send_sem.at[1], cxr_sem.at[q], at_x(q)).wait_recv()
     pl.semaphore_wait(far_sem, 2)
     group = coef.at[pl.ds(base, NXP)]
-    coef_z = [remote(group, group, czs_sem.at[q], czr_sem.at[zi], at_z(q)) for q in z_peers]
+    coef_z = [remote(group, group, send_sem.at[2], czr_sem.at[zi], at_z(q)) for q in z_peers]
     for copy in coef_z:
         copy.start()
 
@@ -211,14 +232,19 @@
         mbuf[way, t, 2] = c
         mbuf[way, t, 3] = d
         mbuf[way, t, 4] = jnp.concatenate([scale, scale], axis=0)
+        return scaled((a, b, c, d))
 
     @pl.loop(0, 2)
     def _(way):
         for j in range(NXP):
             block_product(base + j, way)
 
-    for q in gx_peers:
-        remote(sbuf.at[q], rbuf.at[q], fs_sem.at[q], fr_sem.at[q], at_gx(q)).wait_recv()
+    def wait_for(ref, sem):
+        pltpu.make_async_copy(ref, ref, sem).wait()
+
+    wait_for(rbuf.at[pl.ds(0, PLANES - 1)], recv_sem.at[0])
+    loads[4].wait()
+    loads[5].wait()
     values = []
     for a in range(RADIX):
         at = (a % 2) * 32
@@ -230,7 +256,7 @@
         ure[pl.ds(k, ROWS, stride=RADIX), :] = re * c + im * s
         uim[pl.ds(k, ROWS, stride=RADIX), :] = im * c - re * s
     both = jnp.concatenate([ure[...], uim[...]], axis=1)
-    spec[...] = jnp.dot(both, matrix[...], precision=HIGHEST, preferred_element_type=jnp.float32)
+    spec[...] = product(both, matrix[...])
 
     def rhs(i, part):
         return spec[i * RADIX : (i + 1) * RADIX, part * LANES : (part + 1) * LANES]
@@ -242,39 +268,49 @@
                 r = rhs(i, part) * alone[2 * way + 1, i]
                 y = -r if y is None else alone[2 * way, i] * y - r
             raw[xi, (2 * way + part) * RADIX : (2 * way + part + 1) * RADIX, :] = y
-    to_x = [remote(raw.at[xi], raw.at[xi], xs_sem.at[q], xr_sem.at[xi], at_x(q)) for q in x_peers]
+    to_x = [remote(raw.at[xi], raw.at[xi], send_sem.at[3], recv_sem.at[1], at_x(q)) for q in x_peers]
     for copy in to_x:
         copy.start()
+
+    for slot in range(4):
+        for k in range(4):
+            chain[slot, k] = jnp.zeros_like(one) if k in (1, 2) else one
 
     @pl.loop(0, NZ - 1)
     def _(n):
         step = n // 2 + 1
         q = lax.rem(zi + jnp.where(n % 2 == 0, step, NZ - step), NZ)
         there = coef.at[pl.ds(q * NXP, NXP)]
-        remote(there, there, czs_sem.at[q], czr_sem.at[q], at_z(q)).wait_recv()
+        remote(there, there, send_sem.at[2], czr_sem.at[q], at_z(q)).wait_recv()
+        way = (q > zi).astype(jnp.int32)
+        far = jnp.logical_xor(way == 1, n % 2 == 0)
+        slot = way + 2 * far.astype(jnp.int32)
+        whole = None
         for j in range(NXP):
-            block_product(q * NXP + j, (q > zi).astype(jnp.int32))
-
-    gbuf[...] = jnp.zeros_like(gbuf)
-
-    def advance(t, way):
-        g = gbuf[way]
+            this = block_product(q * NXP + jnp.where(way == 0, j, NXP - 1 - j), way)
+            whole = this if whole is None else times(this, whole)
+        old = tuple(chain[slot, k] for k in range(4))
+        outer = tuple(jnp.where(far, w, o) for w, o in zip(whole, old))
+        inner = tuple(jnp.where(far, o, w) for w, o in zip(whole, old))
+        for k, v in enumerate(scaled(times(outer, inner))):
+            chain[slot, k] = v
+
+    def advance(t, way, g):
         inv = 1.0 / (mbuf[way, t, 2] * g + mbuf[way, t, 3])
-        gbuf[way] = (mbuf[way, t, 0] * g + mbuf[way, t, 1]) * inv
         abuf[way, t] = mbuf[way, t, 4] * inv
-        return g
-
-    @pl.loop(0, BLOCKS - NXP)
-    def _(n):
-        above = (n >= base).astype(jnp.int32)
-        advance(jnp.where(n < base, n, BLOCKS - 1 - (n - base)), above)
-
+        return (mbuf[way, t, 0] * g + mbuf[way, t, 1]) * inv
+
+    enter = []
+    for way in range(2):
+        top, bottom = chain[way + 2, 1], chain[way + 2, 3]
+        enter.append((chain[way, 0] * top + chain[way, 1] * bottom) / (chain[way, 2] * top + chain[way, 3] * bottom))
     for j in range(NXP):
-        gin[0, j] = advance(base + j, 0)
-        gin[1, NXP - 1 - j] = advance(base + NXP - 1 - j, 1)
-
-    for q in x_peers:
-        remote(raw.at[q], raw.at[q], xs_sem.at[q], xr_sem.at[q], at_x(q)).wait_recv()
+        for way in range(2):
+            t = j if way == 0 else NXP - 1 - j
+            gin[way, t] = enter[way]
+            enter[way] = advance(base + t, way, enter[way])
+
+    wait_for(raw.at[pl.ds(0, NXP - 1)], recv_sem.at[1])
     entering = []
     for way, order in enumerate((range(NXP), range(NXP - 1, -1, -1))):
         run, mine = [jnp.zeros_like(one)] * 2, [jnp.zeros_like(one)] * 2
@@ -294,9 +330,16 @@
     to_z = []
     for q in z_peers:
         which = jnp.where(q > zi, 0, 1)
-        to_z.append(remote(gz.at[which], zrecv.at[zi], zs_sem.at[q], zr_sem.at[zi], at_z(q)))
+        to_z.append(remote(gz.at[which], zrecv.at[zi], send_sem.at[4], recv_sem.at[2], at_z(q)))
     for copy in to_z:
         copy.start()
+
+    gbuf[...] = jnp.zeros_like(gbuf)
+
+    @pl.loop(0, BLOCKS - NXP)
+    def _(n):
+        way = (n >= base).astype(jnp.int32)
+        gbuf[way] = advance(jnp.where(n < base, n, BLOCKS - 1 - (n - base)), way, gbuf[way])
 
     def down(n, run):
         t = gy - 1 - n
@@ -328,8 +371,8 @@
 
     sy = [jnp.zeros_like(one)] * 2
     sz = [jnp.zeros_like(one)] * 2
-    for q in z_peers[::-1]:
-        remote(gz.at[0], zrecv.at[q], zs_sem.at[q], zr_sem.at[q], at_z(q)).wait_recv()
+    wait_for(zrecv.at[pl.ds(0, NZ - 1)], recv_sem.at[2])
+    for q in z_peers:
         lower_side = q < zi
         w = wbuf[q * NXP + jnp.where(lower_side, NXP - 1, 0)]
         wy = jnp.where(lower_side, w, 0.0)
@@ -354,11 +397,10 @@
                 x = factors[2, i] * x + ends[part][i]
             ref[i * RADIX : (i + 1) * RADIX, :] = x
 
-    both = jnp.concatenate([ure[...], uim[...]], axis=1)
-    back = lax.dot_general(both, matrix[...], (((1,), (1,)), ((), ())), precision=HIGHEST,
-                           preferred_element_type=jnp.float32)
-    ure[...] = back[:, :LANES]
-    uim[...] = back[:, LANES:]
+    both = jnp.concatenate([uim[...], ure[...]], axis=1)
+    back = product(both, matrix[...])
+    uim[...] = back[:, :LANES]
+    ure[...] = back[:, LANES:]
     values = []
     for k in range(RADIX):
         re = ure[pl.ds(k, ROWS, stride=RADIX), :]
@@ -371,18 +413,19 @@
         at = (a % 2) * 32
         obuf[a // 2, at : at + ROWS, :] = values[a][0]
         obuf[a // 2, at + ROWS : at + 2 * ROWS, :] = values[a][1]
-    backward = [remote(obuf.at[q], fbuf.at[gx], bs_sem.at[q], br_sem.at[gx], at_gx(q)) for q in gx_peers]
+    backward = [remote(obuf.at[q], fbuf.at[gx], send_sem.at[5], recv_sem.at[3], at_gx(q)) for q in gx_peers]
     for copy in backward:
         copy.start()
     own = pltpu.make_async_copy(obuf.at[gx], fbuf.at[gx], load_sem.at[0])
     own.start()
-    for copy in coef_x + forward + coef_z + to_z + to_x:
-        copy.wait_send()
+    wait_for(sbuf.at[pl.ds(0, PLANES - 1)], send_sem.at[0])
+    wait_for(coef.at[pl.ds(0, NXP - 1)], send_sem.at[1])
+    wait_for(coef.at[pl.ds(0, NXP * (NZ - 1))], send_sem.at[2])
+    wait_for(raw.at[pl.ds(0, NXP - 1)], send_sem.at[3])
+    wait_for(zrecv.at[pl.ds(0, NZ - 1)], send_sem.at[4])
     own.wait()
-    for q in gx_peers:
-        remote(obuf.at[q], fbuf.at[q], bs_sem.at[q], br_sem.at[q], at_gx(q)).wait_recv()
-    for copy in backward:
-        copy.wait_send()
+    wait_for(obuf.at[pl.ds(0, PLANES - 1)], send_sem.at[5])
+    wait_for(fbuf.at[pl.ds(0, PLANES - 1)], recv_sem.at[3])
 
 
 def assemble(fbuf, out):
@@ -400,21 +443,23 @@
     vmem = lambda *shape: pltpu.VMEM(shape, f32)
     smem = lambda *shape: pltpu.SMEM(shape, f32)
     any_spec = pl.BlockSpec(memory_space=pl.ANY)
+    shape = source.shape
+    source = source.reshape(ROWS, 2, PLANES, 2, LANES).transpose(0, 1, 3, 2, 4).reshape(4 * ROWS * PLANES, LANES)
     planes = pl.pallas_call(
         kernel,
         out_shape=jax.ShapeDtypeStruct((PLANES, 64, LANES), f32),
         in_specs=[pl.BlockSpec(memory_space=pltpu.HBM)] * 6,
         out_specs=any_spec,
         scratch_shapes=[
-            vmem(2, 2, ROWS, PLANES, LANES), vmem(PLANES, 64, LANES), vmem(PLANES, 64, LANES),
-            vmem(256, LANES), vmem(256, LANES), vmem(256, 256), vmem(256, 256), vmem(2 * RADIX, LANES),
+            vmem(4 * ROWS * PLANES, LANES), vmem(PLANES, 64, LANES), vmem(PLANES, 64, LANES),
+            vmem(256, LANES), vmem(256, LANES), vmem(256, 256),
+            pltpu.VMEM((6 * 256, 256), jnp.bfloat16), vmem(2 * RADIX, LANES),
             smem(ROWS), smem(ROWS), smem(PLANES),
             vmem(BLOCKS, 1, LANES), vmem(2, BLOCKS, 5, RADIX, LANES), vmem(2, BLOCKS, RADIX, LANES),
-            vmem(BLOCKS, RADIX, LANES), vmem(2, RADIX, LANES), vmem(2, NXP, RADIX, LANES),
+            vmem(BLOCKS, RADIX, LANES), vmem(2, RADIX, LANES), vmem(2, NXP, RADIX, LANES), vmem(4, 4, RADIX, LANES),
             vmem(4, ROWS, RADIX, LANES), vmem(3, ROWS, RADIX, LANES),
             vmem(NXP, 64, LANES), vmem(2, 32, LANES), vmem(NZ, 32, LANES), vmem(PLANES, 64, LANES),
-            dma((9,)), dma((PLANES,)), dma((PLANES,)), dma((NXP,)), dma((NXP,)), dma((NZ,)), dma((NZ,)),
-            dma((NZ,)), dma((NZ,)), dma((NXP,)), dma((NXP,)), dma((PLANES,)), dma((PLANES,)),
+            dma((6,)), dma((6,)), dma((4,)), dma((NXP,)), dma((NZ,)),
             pltpu.SemaphoreType.REGULAR, pltpu.SemaphoreType.REGULAR,
         ],
         compiler_params=pltpu.CompilerParams(
@@ -429,7 +474,7 @@
         compiler_params=pltpu.CompilerParams(vmem_limit_bytes=4 * 1024 * 1024),
     )(planes)
     result = result.reshape(ROWS, 2, 2, PLANES, LANES)
-    return result.transpose(0, 1, 3, 2, 4).reshape(source.shape)
+    return result.transpose(0, 1, 3, 2, 4).reshape(shape)
 
 
 def solution(mesh):

time: 32.6 us -> 32.5 us (level)
  no operation moved by 1% of the time
where the time goes in v2:
time: 32.5 us; the launch traced here: 32.4 us
  Pallas kernels  32.4 us (100%)
    pallas_call x1, Pallas kernels, local(): pl.pallas_call(kernel, out_shape=jax.ShapeDtypeStruct((PLANES, 64, LANES)...  31.5 us
    pallas_call x1, Pallas kernels, local(): pl.pallas_call(assemble, out_shape=jax.ShapeDtypeStruct((ROWS * 4 * PLANE...  0.91 us

profile of v2, /device:TPU:1, one launch (start us, length us, event | category | flops | bytes accessed | tf_op | source)
XLA Modules:
  0.0 32.4 jit_solution(16558554156418369370)
XLA Ops:
  0.0 31.5 %shard_map.64.fbuf = f32[8,64,128]{2,1,0:T(8,128)S(1)} custom-call(f32[512,128]{1,0:T(8,128)} %bitcast.10, f32[16]{0:T(128)} %lower_hbm.1, f32[16]{0:T(128)} %upper_hbm.1, f32[8]{0:T(128)} %span_hbm.1, bf16[1536,256]{1,0:T(8,128)(2,1)} %constant.4.clone.matrix_hbm, f32[32,128]{1,0:T(8,128)} %constant.5.clone.twiddle_hbm), custom_call_target="tpu_custom_call" | custom-call | tf_op jit(solution)/shard_map/pallas_call | solution.py:448
  31.5 0.9 %shard_map.65 = f32[512,128]{1,0:T(8,128)} custom-call(f32[8,64,128]{2,1,0:T(8,128)S(1)} %shard_map.64.fbuf), custom_call_target="tpu_custom_call" | custom-call | tf_op jit(solution)/shard_map/pallas_call | solution.py:469

commit v3 on v2

--- a/solution.py
+++ b/solution.py
@@ -19,6 +19,7 @@
 NZ = 8
 NXP = 4
 BLOCKS = NZ * NXP
+HALF = RADIX // 2 + 1
 
 
 def transform_constants():
@@ -82,10 +83,23 @@
     return tuple(v * r for v in x)
 
 
+def mirrored(x):
+    sub = lax.broadcasted_iota(jnp.int32, (8, LANES), 0)
+    lane = lax.broadcasted_iota(jnp.int32, (8, LANES), 1)
+    top = x[0:8, :]
+    turned = jnp.take_along_axis(top, LANES - 1 - lane, axis=1)
+    turned = jnp.take_along_axis(turned, (8 - sub) % 8, axis=0)
+    return jnp.concatenate([top, jnp.where(sub == 0, x[8:16, :], turned)], axis=0)
+
+
+def transposed(k):
+    return pl.ds((k // 8) * 8 * ROWS + k % 8, ROWS, stride=8)
+
+
 def kernel(
     source, lower_hbm, upper_hbm, span_hbm, matrix_hbm, twiddle_hbm, fbuf,
     src, sbuf, rbuf, ure, uim, spec, matrix, twiddle, lower, upper, span,
-    coef, mbuf, abuf, wbuf, gbuf, gin, chain, alone, factors,
+    coef, splats, kbuf, own_products, groups, abuf, wbuf, gbuf, gin, chain, alone, factors,
     raw, gz, zrecv, obuf,
     load_sem, send_sem, recv_sem, cxr_sem, czr_sem, near_sem, far_sem,
 ):
@@ -125,10 +139,7 @@
 
     loads[0].wait()
     for q in range(PLANES):
-        for xt in range(2):
-            for part in range(2):
-                at = (xt * 2 + part) * ROWS
-                sbuf[q, at : at + ROWS, :] = src[pl.ds((part * 2 + xt) * PLANES + q, ROWS, stride=4 * PLANES), :]
+        sbuf[q] = src[pl.ds(q, 4 * ROWS, stride=PLANES), :]
 
     pl.semaphore_wait(barrier, len(near))
 
@@ -203,41 +214,41 @@
     for copy in coef_z:
         copy.start()
 
-    def block_product(t, way):
-        row = jnp.broadcast_to(coef[t], (8, LANES))
-        turned = pltpu.roll(row, LANES // 2, 1)
-        row = jnp.where(way == 0, row, turned)
-
-        def splat(i):
-            one = jnp.broadcast_to(row[:, i : i + 1], (8, LANES))
-            return one, jnp.concatenate([one, one], axis=0)
-
+    kbuf[...] = kappa
+
+    def block_products(blocks, ways, finish):
+        rows = jnp.concatenate([coef[t] for t in blocks], axis=0)
+        sub = lax.broadcasted_iota(jnp.int32, (8, LANES), 0)
+        turn = jnp.where(sub < NXP, ways[0], ways[1]) == 1
+        rows = jnp.where(turn, pltpu.roll(rows, LANES // 2, 1), rows)
         scale = None
-        for i in range(ROWS):
-            one, l = splat(i)
-            _, u = splat(ROWS + i)
-            _, total = splat(2 * ROWS + i)
-            _, gained = splat(3 * ROWS + i)
-            rounded = ((total + kappa) - total) + gained
-            if i == 0:
-                scale, a, b, c, d = one, l, rounded, l, u + rounded
-                continue
-            scale = scale * one
-            a = l * a + rounded * c
-            b = l * b + rounded * d
-            c = a + u * c
-            d = b + u * d
-        mbuf[way, t, 0] = a
-        mbuf[way, t, 1] = b
-        mbuf[way, t, 2] = c
-        mbuf[way, t, 3] = d
-        mbuf[way, t, 4] = jnp.concatenate([scale, scale], axis=0)
-        return scaled((a, b, c, d))
-
-    @pl.loop(0, 2)
-    def _(way):
-        for j in range(NXP):
-            block_product(base + j, way)
+        for k in range(4 * ROWS):
+            one = jnp.broadcast_to(rows[:, k : k + 1], (8, LANES))
+            splats[k] = one
+            if k < ROWS:
+                scale = one if scale is None else scale * one
+        for k in range(0, HALF, 3):
+            waves = [jnp.broadcast_to(kbuf[n : n + 1, :], (8, LANES)) for n in range(k, k + 3)]
+            state = [None] * 3
+            for i in range(ROWS):
+                l, u, total, gained = [splats[n * ROWS + i] for n in range(4)]
+                for n in range(3):
+                    rounded = ((total + waves[n]) - total) + gained
+                    if i == 0:
+                        state[n] = (l, rounded, l, u + rounded)
+                        continue
+                    a, b, c, d = state[n]
+                    a = l * a + rounded * c
+                    b = l * b + rounded * d
+                    state[n] = (a, b, a + u * c, b + u * d)
+            for n in range(3):
+                finish(k + n, scaled(state[n] + (scale,)))
+
+    def keep_own(k, values):
+        for n, v in enumerate(values):
+            own_products[n, 8 * k : 8 * k + 8, :] = v
+
+    block_products([base + j for j in range(NXP)] * 2, (0, 1), keep_own)
 
     def wait_for(ref, sem):
         pltpu.make_async_copy(ref, ref, sem).wait()
@@ -247,19 +258,19 @@
     loads[5].wait()
     values = []
     for a in range(RADIX):
-        at = (a % 2) * 32
-        values.append((rbuf[a // 2, at : at + ROWS, :], rbuf[a // 2, at + ROWS : at + 2 * ROWS, :]))
+        values.append(tuple(rbuf[a // 2, pl.ds(2 * part + a % 2, ROWS, stride=4), :] for part in range(2)))
     values = butterflies(values, False)
     for k in range(RADIX):
         re, im = values[k]
         c, s = twiddle[k : k + 1, :], twiddle[RADIX + k : RADIX + k + 1, :]
-        ure[pl.ds(k, ROWS, stride=RADIX), :] = re * c + im * s
-        uim[pl.ds(k, ROWS, stride=RADIX), :] = im * c - re * s
+        ure[transposed(k), :] = re * c + im * s
+        uim[transposed(k), :] = im * c - re * s
     both = jnp.concatenate([ure[...], uim[...]], axis=1)
     spec[...] = product(both, matrix[...])
 
     def rhs(i, part):
-        return spec[i * RADIX : (i + 1) * RADIX, part * LANES : (part + 1) * LANES]
+        lanes = slice(part * LANES, (part + 1) * LANES)
+        return jnp.concatenate([spec[h * 128 + i * 8 : h * 128 + i * 8 + 8, lanes] for h in range(2)], axis=0)
 
     for way, order in enumerate((range(ROWS), range(ROWS - 1, -1, -1))):
         for part in range(2):
@@ -276,29 +287,51 @@
         for k in range(4):
             chain[slot, k] = jnp.zeros_like(one) if k in (1, 2) else one
 
-    @pl.loop(0, NZ - 1)
+    def next_block(x, shift):
+        return tuple(pltpu.roll(v, 8 - shift, 0) for v in x)
+
+    @pl.loop(0, NZ // 2)
     def _(n):
-        step = n // 2 + 1
-        q = lax.rem(zi + jnp.where(n % 2 == 0, step, NZ - step), NZ)
-        there = coef.at[pl.ds(q * NXP, NXP)]
-        remote(there, there, send_sem.at[2], czr_sem.at[q], at_z(q)).wait_recv()
-        way = (q > zi).astype(jnp.int32)
-        far = jnp.logical_xor(way == 1, n % 2 == 0)
-        slot = way + 2 * far.astype(jnp.int32)
-        whole = None
-        for j in range(NXP):
-            this = block_product(q * NXP + jnp.where(way == 0, j, NXP - 1 - j), way)
-            whole = this if whole is None else times(this, whole)
-        old = tuple(chain[slot, k] for k in range(4))
-        outer = tuple(jnp.where(far, w, o) for w, o in zip(whole, old))
-        inner = tuple(jnp.where(far, o, w) for w, o in zip(whole, old))
-        for k, v in enumerate(scaled(times(outer, inner))):
-            chain[slot, k] = v
-
-    def advance(t, way, g):
-        inv = 1.0 / (mbuf[way, t, 2] * g + mbuf[way, t, 3])
-        abuf[way, t] = mbuf[way, t, 4] * inv
-        return (mbuf[way, t, 0] * g + mbuf[way, t, 1]) * inv
+        pair = (lax.rem(zi + n + 1, NZ), lax.rem(zi + NZ - 1 - n, NZ))
+        ways = [(q > zi).astype(jnp.int32) for q in pair]
+
+        def arrive(q):
+            there = coef.at[pl.ds(q * NXP, NXP)]
+            remote(there, there, send_sem.at[2], czr_sem.at[q], at_z(q)).wait_recv()
+
+        arrive(pair[0])
+
+        @pl.when(n < NZ // 2 - 1)
+        def _():
+            arrive(pair[1])
+
+        def keep_groups(k, values):
+            for shift in (1, 2):
+                later = next_block(values, shift)
+                values = times(later[:4], values[:4]) + (later[4] * values[4],)
+            values = scaled(values)
+            for m, v in enumerate(values):
+                for g in range(2):
+                    groups[pair[g], m, k : k + 1, :] = v[NXP * g : NXP * g + 1, :]
+
+        blocks = [q * NXP + jnp.where(w == 0, j, NXP - 1 - j) for q, w in zip(pair, ways) for j in range(NXP)]
+        block_products(blocks, ways, keep_groups)
+
+        def join(g):
+            far = ways[g] != 1 - g
+            slot = ways[g] + 2 * far.astype(jnp.int32)
+            whole = tuple(groups[pair[g], k] for k in range(4))
+            old = tuple(chain[slot, k] for k in range(4))
+            outer = tuple(jnp.where(far, w, o) for w, o in zip(whole, old))
+            inner = tuple(jnp.where(far, o, w) for w, o in zip(whole, old))
+            for k, v in enumerate(scaled(times(outer, inner))):
+                chain[slot, k] = v
+
+        join(0)
+
+        @pl.when(n < NZ // 2 - 1)
+        def _():
+            join(1)
 
     enter = []
     for way in range(2):
@@ -307,8 +340,12 @@
     for j in range(NXP):
         for way in range(2):
             t = j if way == 0 else NXP - 1 - j
-            gin[way, t] = enter[way]
-            enter[way] = advance(base + t, way, enter[way])
+            g = enter[way]
+            a, b, c, d, scale = [own_products[n, pl.ds(NXP * way + t, RADIX, stride=8), :] for n in range(5)]
+            inv = 1.0 / (c * g + d)
+            gin[way, t] = mirrored(g)
+            abuf[way, t] = mirrored(scale * inv)
+            enter[way] = (a * g + b) * inv
 
     wait_for(raw.at[pl.ds(0, NXP - 1)], recv_sem.at[1])
     entering = []
@@ -316,7 +353,7 @@
         run, mine = [jnp.zeros_like(one)] * 2, [jnp.zeros_like(one)] * 2
         for j in order:
             here = xi == j
-            a = abuf[way, base + j]
+            a = abuf[way, j]
             ae = a * (1.0 - gin[way, j])
             for part in range(2):
                 end = raw[j, (2 * way + part) * RADIX : (2 * way + part + 1) * RADIX, :]
@@ -336,34 +373,34 @@
 
     gbuf[...] = jnp.zeros_like(gbuf)
 
-    @pl.loop(0, BLOCKS - NXP)
+    @pl.loop(0, NZ - 1)
     def _(n):
-        way = (n >= base).astype(jnp.int32)
-        gbuf[way] = advance(jnp.where(n < base, n, BLOCKS - 1 - (n - base)), way, gbuf[way])
-
-    def down(n, run):
-        t = gy - 1 - n
-        wbuf[t] = run
-        return run * abuf[0, t]
+        way = (n >= zi).astype(jnp.int32)
+        q = jnp.where(n < zi, n, NZ - 1 - (n - zi))
+        g = gbuf[way]
+        inv = 1.0 / (groups[q, 2] * g + groups[q, 3])
+        gbuf[way] = (groups[q, 0] * g + groups[q, 1]) * inv
+        wbuf[q] = groups[q, 4] * inv
 
     def below(n, run):
-        t = base - 1 - n
-        wbuf[t] = run
-        return run * abuf[0, t]
-
-    pre = lax.fori_loop(0, xi, down, one)
-    lax.fori_loop(0, base, below, one)
-
-    def up(n, run):
-        return run * abuf[1, gy + 1 + n]
+        q = zi - 1 - n
+        a = wbuf[q]
+        wbuf[q] = mirrored(run)
+        return run * a
+
+    lax.fori_loop(0, zi, below, one)
 
     def above(n, run):
-        t = base + NXP + n
-        wbuf[t] = run
-        return run * abuf[1, t]
-
-    post = lax.fori_loop(0, NXP - 1 - xi, up, one)
-    lax.fori_loop(0, BLOCKS - NXP - base, above, one)
+        q = zi + 1 + n
+        a = wbuf[q]
+        wbuf[q] = mirrored(run)
+        return run * a
+
+    lax.fori_loop(0, NZ - 1 - zi, above, one)
+    pre, post = one, one
+    for j in range(NXP):
+        pre = pre * jnp.where(j < xi, abuf[0, j], 1.0)
+        post = post * jnp.where(j > xi, abuf[1, j], 1.0)
 
     g_end = pivots(range(ROWS), low, upp, gin[0, xi], factors, 0)
     h_in = gin[1, xi]
@@ -374,7 +411,7 @@
     wait_for(zrecv.at[pl.ds(0, NZ - 1)], recv_sem.at[2])
     for q in z_peers:
         lower_side = q < zi
-        w = wbuf[q * NXP + jnp.where(lower_side, NXP - 1, 0)]
+        w = wbuf[q]
         wy = jnp.where(lower_side, w, 0.0)
         wz = jnp.where(lower_side, 0.0, w)
         for part in range(2):
@@ -395,7 +432,8 @@
         for i in range(ROWS - 1, -1, -1):
             if i < ROWS - 1:
                 x = factors[2, i] * x + ends[part][i]
-            ref[i * RADIX : (i + 1) * RADIX, :] = x
+            for h in range(2):
+                ref[h * 128 + i * 8 : h * 128 + i * 8 + 8, :] = x[8 * h : 8 * h + 8, :]
 
     both = jnp.concatenate([uim[...], ure[...]], axis=1)
     back = product(both, matrix[...])
@@ -403,16 +441,15 @@
     ure[...] = back[:, LANES:]
     values = []
     for k in range(RADIX):
-        re = ure[pl.ds(k, ROWS, stride=RADIX), :]
-        im = uim[pl.ds(k, ROWS, stride=RADIX), :]
+        re = ure[transposed(k), :]
+        im = uim[transposed(k), :]
         c = twiddle[k : k + 1, :] * (1.0 / NX)
         s = twiddle[RADIX + k : RADIX + k + 1, :] * (1.0 / NX)
         values.append((re * c - im * s, im * c + re * s))
     values = butterflies(values, True)
     for a in range(RADIX):
-        at = (a % 2) * 32
-        obuf[a // 2, at : at + ROWS, :] = values[a][0]
-        obuf[a // 2, at + ROWS : at + 2 * ROWS, :] = values[a][1]
+        for part in range(2):
+            obuf[a // 2, pl.ds(2 * part + a % 2, ROWS, stride=4), :] = values[a][part]
     backward = [remote(obuf.at[q], fbuf.at[gx], send_sem.at[5], recv_sem.at[3], at_gx(q)) for q in gx_peers]
     for copy in backward:
         copy.start()
@@ -430,10 +467,7 @@
 
 def assemble(fbuf, out):
     for q in range(PLANES):
-        for xt in range(2):
-            for part in range(2):
-                at = (xt * 2 + part) * ROWS
-                out[pl.ds((part * 2 + xt) * PLANES + q, ROWS, stride=4 * PLANES), :] = fbuf[q, at : at + ROWS, :]
+        out[pl.ds(q, 4 * ROWS, stride=PLANES), :] = fbuf[q]
 
 
 def local(source, lower, upper, span):
@@ -455,8 +489,9 @@
             vmem(256, LANES), vmem(256, LANES), vmem(256, 256),
             pltpu.VMEM((6 * 256, 256), jnp.bfloat16), vmem(2 * RADIX, LANES),
             smem(ROWS), smem(ROWS), smem(PLANES),
-            vmem(BLOCKS, 1, LANES), vmem(2, BLOCKS, 5, RADIX, LANES), vmem(2, BLOCKS, RADIX, LANES),
-            vmem(BLOCKS, RADIX, LANES), vmem(2, RADIX, LANES), vmem(2, NXP, RADIX, LANES), vmem(4, 4, RADIX, LANES),
+            vmem(BLOCKS, 1, LANES), vmem(4 * ROWS, 8, LANES), vmem(RADIX, LANES), vmem(5, 8 * RADIX, LANES),
+            vmem(NZ, 5, RADIX, LANES), vmem(2, NXP, RADIX, LANES), vmem(NZ, RADIX, LANES),
+            vmem(2, RADIX, LANES), vmem(2, NXP, RADIX, LANES), vmem(4, 4, RADIX, LANES),
             vmem(4, ROWS, RADIX, LANES), vmem(3, ROWS, RADIX, LANES),
             vmem(NXP, 64, LANES), vmem(2, 32, LANES), vmem(NZ, 32, LANES), vmem(PLANES, 64, LANES),
             dma((6,)), dma((6,)), dma((4,)), dma((NXP,)), dma((NZ,)),

time: 32.5 us -> 30.2 us (0.929)
  Pallas kernels: 32.4 us -> 30.1 us
    pallas_call x1, Pallas kernels: 31.5 us -> 29.4 us  [local(): pl.pallas_call(kernel, out_shape=jax.ShapeDtypeStruct((PLANES, 64, LANES)...]
where the time goes in v3:
time: 30.2 us; the launch traced here: 30.1 us
  Pallas kernels  30.1 us (100%)
    pallas_call x1, Pallas kernels, local(): pl.pallas_call(kernel, out_shape=jax.ShapeDtypeStruct((PLANES, 64, LANES)...  29.4 us
    pallas_call x1, Pallas kernels, local(): pl.pallas_call(assemble, out_shape=jax.ShapeDtypeStruct((ROWS * 4 * PLANE...  0.76 us

profile of v3, /device:TPU:1, one launch (start us, length us, event | category | flops | bytes accessed | tf_op | source)
XLA Modules:
  0.0 30.1 jit_solution(2797129507736998093)
XLA Ops:
  0.0 29.4 %shard_map.64.fbuf = f32[8,64,128]{2,1,0:T(8,128)S(1)} custom-call(f32[512,128]{1,0:T(8,128)} %bitcast.10, f32[16]{0:T(128)} %lower_hbm.1, f32[16]{0:T(128)} %upper_hbm.1, f32[8]{0:T(128)} %span_hbm.1, bf16[1536,256]{1,0:T(8,128)(2,1)} %constant.4.clone.matrix_hbm, f32[32,128]{1,0:T(8,128)} %constant.5.clone.twiddle_hbm), custom_call_target="tpu_custom_call" | custom-call | tf_op jit(solution)/shard_map/pallas_call | solution.py:482
  29.4 0.8 %shard_map.65 = f32[512,128]{1,0:T(8,128)} custom-call(f32[8,64,128]{2,1,0:T(8,128)S(1)} %shard_map.64.fbuf), custom_call_target="tpu_custom_call" | custom-call | tf_op jit(solution)/shard_map/pallas_call | solution.py:504

commit v4 on v3

--- a/solution.py
+++ b/solution.py
@@ -92,8 +92,8 @@
     return jnp.concatenate([top, jnp.where(sub == 0, x[8:16, :], turned)], axis=0)
 
 
-def transposed(k):
-    return pl.ds((k // 8) * 8 * ROWS + k % 8, ROWS, stride=8)
+def transposed(o, k):
+    return pl.ds(o * 128 + (k // 8) * 64 + k % 8, 8, stride=8)
 
 
 def kernel(
@@ -101,7 +101,7 @@
     src, sbuf, rbuf, ure, uim, spec, matrix, twiddle, lower, upper, span,
     coef, splats, kbuf, own_products, groups, abuf, wbuf, gbuf, gin, chain, alone, factors,
     raw, gz, zrecv, obuf,
-    load_sem, send_sem, recv_sem, cxr_sem, czr_sem, near_sem, far_sem,
+    load_sem, send_sem, recv_sem, arrived, cxr_sem, czr_sem, near_sem, far_sem,
 ):
     gx = lax.axis_index("gx")
     gy = lax.axis_index("gy")
@@ -148,9 +148,12 @@
             src_ref=src_ref, dst_ref=dst_ref, send_sem=send, recv_sem=recv,
             device_id=device, device_id_type=MESH)
 
-    forward = [remote(sbuf.at[q], rbuf.at[gx], send_sem.at[0], recv_sem.at[0], at_gx(q)) for q in gx_peers]
-    for copy in forward:
-        copy.start()
+    def octet(ref, q, o):
+        return ref.at[q, pl.ds(32 * o, 32)]
+
+    for o in range(2):
+        for q in gx_peers:
+            remote(octet(sbuf, q, o), octet(rbuf, gx, o), send_sem.at[0], arrived.at[o], at_gx(q)).start()
     for q in z_near:
         pl.semaphore_signal(near_sem, inc=1, device_id=at_z(q), device_id_type=MESH)
     rbuf[gx] = sbuf[gx]
@@ -253,24 +256,30 @@
     def wait_for(ref, sem):
         pltpu.make_async_copy(ref, ref, sem).wait()
 
-    wait_for(rbuf.at[pl.ds(0, PLANES - 1)], recv_sem.at[0])
-    loads[4].wait()
-    loads[5].wait()
-    values = []
-    for a in range(RADIX):
-        values.append(tuple(rbuf[a // 2, pl.ds(2 * part + a % 2, ROWS, stride=4), :] for part in range(2)))
-    values = butterflies(values, False)
-    for k in range(RADIX):
-        re, im = values[k]
-        c, s = twiddle[k : k + 1, :], twiddle[RADIX + k : RADIX + k + 1, :]
-        ure[transposed(k), :] = re * c + im * s
-        uim[transposed(k), :] = im * c - re * s
-    both = jnp.concatenate([ure[...], uim[...]], axis=1)
-    spec[...] = product(both, matrix[...])
+    def wait_for_octet(ref, sem):
+        wait_for(ref.at[pl.ds(0, PLANES - 1), pl.ds(0, 32)], sem)
+
+    for o in range(2):
+        wait_for_octet(rbuf, arrived.at[o])
+        if o == 0:
+            loads[4].wait()
+            loads[5].wait()
+        values = []
+        for a in range(RADIX):
+            values.append(tuple(rbuf[a // 2, pl.ds(32 * o + 2 * part + a % 2, 8, stride=4), :] for part in range(2)))
+        values = butterflies(values, False)
+        for k in range(RADIX):
+            re, im = values[k]
+            c, s = twiddle[k : k + 1, :], twiddle[RADIX + k : RADIX + k + 1, :]
+            ure[transposed(o, k), :] = re * c + im * s
+            uim[transposed(o, k), :] = im * c - re * s
+        rows = slice(128 * o, 128 * o + 128)
+        spec[rows, :] = product(jnp.concatenate([ure[rows, :], uim[rows, :]], axis=1), matrix[...])
 
     def rhs(i, part):
         lanes = slice(part * LANES, (part + 1) * LANES)
-        return jnp.concatenate([spec[h * 128 + i * 8 : h * 128 + i * 8 + 8, lanes] for h in range(2)], axis=0)
+        at = [(i // 8) * 128 + h * 64 + (i % 8) * 8 for h in range(2)]
+        return jnp.concatenate([spec[n : n + 8, lanes] for n in at], axis=0)
 
     for way, order in enumerate((range(ROWS), range(ROWS - 1, -1, -1))):
         for part in range(2):
@@ -279,7 +288,7 @@
                 r = rhs(i, part) * alone[2 * way + 1, i]
                 y = -r if y is None else alone[2 * way, i] * y - r
             raw[xi, (2 * way + part) * RADIX : (2 * way + part + 1) * RADIX, :] = y
-    to_x = [remote(raw.at[xi], raw.at[xi], send_sem.at[3], recv_sem.at[1], at_x(q)) for q in x_peers]
+    to_x = [remote(raw.at[xi], raw.at[xi], send_sem.at[3], recv_sem.at[0], at_x(q)) for q in x_peers]
     for copy in to_x:
         copy.start()
 
@@ -347,7 +356,7 @@
             abuf[way, t] = mirrored(scale * inv)
             enter[way] = (a * g + b) * inv
 
-    wait_for(raw.at[pl.ds(0, NXP - 1)], recv_sem.at[1])
+    wait_for(raw.at[pl.ds(0, NXP - 1)], recv_sem.at[0])
     entering = []
     for way, order in enumerate((range(NXP), range(NXP - 1, -1, -1))):
         run, mine = [jnp.zeros_like(one)] * 2, [jnp.zeros_like(one)] * 2
@@ -367,7 +376,7 @@
     to_z = []
     for q in z_peers:
         which = jnp.where(q > zi, 0, 1)
-        to_z.append(remote(gz.at[which], zrecv.at[zi], send_sem.at[4], recv_sem.at[2], at_z(q)))
+        to_z.append(remote(gz.at[which], zrecv.at[zi], send_sem.at[4], recv_sem.at[1], at_z(q)))
     for copy in to_z:
         copy.start()
 
@@ -408,7 +417,7 @@
 
     sy = [jnp.zeros_like(one)] * 2
     sz = [jnp.zeros_like(one)] * 2
-    wait_for(zrecv.at[pl.ds(0, NZ - 1)], recv_sem.at[2])
+    wait_for(zrecv.at[pl.ds(0, NZ - 1)], recv_sem.at[1])
     for q in z_peers:
         lower_side = q < zi
         w = wbuf[q]
@@ -425,34 +434,36 @@
         for i in range(ROWS):
             y = factors[0, i] * y - factors[1, i] * rhs(i, part)
             ends[part].append(y)
+    solved = []
     for part in range(2):
-        ref = uim if part else ure
         z_in = entering[1][part] + post * sz[part]
-        x = (factors[2, ROWS - 1] * z_in + ends[part][-1]) * scale
-        for i in range(ROWS - 1, -1, -1):
-            if i < ROWS - 1:
-                x = factors[2, i] * x + ends[part][i]
-            for h in range(2):
-                ref[h * 128 + i * 8 : h * 128 + i * 8 + 8, :] = x[8 * h : 8 * h + 8, :]
-
-    both = jnp.concatenate([uim[...], ure[...]], axis=1)
-    back = product(both, matrix[...])
-    uim[...] = back[:, :LANES]
-    ure[...] = back[:, LANES:]
-    values = []
-    for k in range(RADIX):
-        re = ure[transposed(k), :]
-        im = uim[transposed(k), :]
-        c = twiddle[k : k + 1, :] * (1.0 / NX)
-        s = twiddle[RADIX + k : RADIX + k + 1, :] * (1.0 / NX)
-        values.append((re * c - im * s, im * c + re * s))
-    values = butterflies(values, True)
-    for a in range(RADIX):
-        for part in range(2):
-            obuf[a // 2, pl.ds(2 * part + a % 2, ROWS, stride=4), :] = values[a][part]
-    backward = [remote(obuf.at[q], fbuf.at[gx], send_sem.at[5], recv_sem.at[3], at_gx(q)) for q in gx_peers]
-    for copy in backward:
-        copy.start()
+        solved.append((factors[2, ROWS - 1] * z_in + ends[part][-1]) * scale)
+
+    for o in (1, 0):
+        for i in range(8 * o + 7, 8 * o - 1, -1):
+            for part, ref in enumerate((ure, uim)):
+                if i < ROWS - 1:
+                    solved[part] = factors[2, i] * solved[part] + ends[part][i]
+                for h in range(2):
+                    at = o * 128 + h * 64 + (i % 8) * 8
+                    ref[at : at + 8, :] = solved[part][8 * h : 8 * h + 8, :]
+        rows = slice(128 * o, 128 * o + 128)
+        back = product(jnp.concatenate([uim[rows, :], ure[rows, :]], axis=1), matrix[...])
+        uim[rows, :] = back[:, :LANES]
+        ure[rows, :] = back[:, LANES:]
+        values = []
+        for k in range(RADIX):
+            re = ure[transposed(o, k), :]
+            im = uim[transposed(o, k), :]
+            c = twiddle[k : k + 1, :] * (1.0 / NX)
+            s = twiddle[RADIX + k : RADIX + k + 1, :] * (1.0 / NX)
+            values.append((re * c - im * s, im * c + re * s))
+        values = butterflies(values, True)
+        for a in range(RADIX):
+            for part in range(2):
+                obuf[a // 2, pl.ds(32 * o + 2 * part + a % 2, 8, stride=4), :] = values[a][part]
+        for q in gx_peers:
+            remote(octet(obuf, q, o), octet(fbuf, gx, o), send_sem.at[5], arrived.at[2 + o], at_gx(q)).start()
     own = pltpu.make_async_copy(obuf.at[gx], fbuf.at[gx], load_sem.at[0])
     own.start()
     wait_for(sbuf.at[pl.ds(0, PLANES - 1)], send_sem.at[0])
@@ -462,7 +473,8 @@
     wait_for(zrecv.at[pl.ds(0, NZ - 1)], send_sem.at[4])
     own.wait()
     wait_for(obuf.at[pl.ds(0, PLANES - 1)], send_sem.at[5])
-    wait_for(fbuf.at[pl.ds(0, PLANES - 1)], recv_sem.at[3])
+    for o in range(2):
+        wait_for_octet(fbuf, arrived.at[2 + o])
 
 
 def assemble(fbuf, out):
@@ -494,7 +506,7 @@
             vmem(2, RADIX, LANES), vmem(2, NXP, RADIX, LANES), vmem(4, 4, RADIX, LANES),
             vmem(4, ROWS, RADIX, LANES), vmem(3, ROWS, RADIX, LANES),
             vmem(NXP, 64, LANES), vmem(2, 32, LANES), vmem(NZ, 32, LANES), vmem(PLANES, 64, LANES),
-            dma((6,)), dma((6,)), dma((4,)), dma((NXP,)), dma((NZ,)),
+            dma((6,)), dma((6,)), dma((2,)), dma((4,)), dma((NXP,)), dma((NZ,)),
             pltpu.SemaphoreType.REGULAR, pltpu.SemaphoreType.REGULAR,
         ],
         compiler_params=pltpu.CompilerParams(

time: 30.2 us -> 30.1 us (level)
  no operation moved by 1% of the time
where the time goes in v4:
time: 30.1 us; the launch traced here: 30 us
  Pallas kernels  30 us (100%)
    pallas_call x1, Pallas kernels, local(): pl.pallas_call(kernel, out_shape=jax.ShapeDtypeStruct((PLANES, 64, LANES)...  29.2 us
    pallas_call x1, Pallas kernels, local(): pl.pallas_call(assemble, out_shape=jax.ShapeDtypeStruct((ROWS * 4 * PLANE...  0.76 us

profile of v4, /device:TPU:1, one launch (start us, length us, event | category | flops | bytes accessed | tf_op | source)
XLA Modules:
  0.0 30.0 jit_solution(10203196182656992402)
XLA Ops:
  0.0 29.2 %shard_map.64.fbuf = f32[8,64,128]{2,1,0:T(8,128)S(1)} custom-call(f32[512,128]{1,0:T(8,128)} %bitcast.10, f32[16]{0:T(128)} %lower_hbm.1, f32[16]{0:T(128)} %upper_hbm.1, f32[8]{0:T(128)} %span_hbm.1, bf16[1536,256]{1,0:T(8,128)(2,1)} %constant.4.clone.matrix_hbm, f32[32,128]{1,0:T(8,128)} %constant.5.clone.twiddle_hbm), custom_call_target="tpu_custom_call" | custom-call | tf_op jit(solution)/shard_map/pallas_call | solution.py:494
  29.2 0.8 %shard_map.65 = f32[512,128]{1,0:T(8,128)} custom-call(f32[8,64,128]{2,1,0:T(8,128)S(1)} %shard_map.64.fbuf), custom_call_target="tpu_custom_call" | custom-call | tf_op jit(solution)/shard_map/pallas_call | solution.py:516

commit v5 on v4

--- a/solution.py
+++ b/solution.py
@@ -20,6 +20,7 @@
 NXP = 4
 BLOCKS = NZ * NXP
 HALF = RADIX // 2 + 1
+PARTS = 4
 
 
 def transform_constants():
@@ -99,7 +100,7 @@
 def kernel(
     source, lower_hbm, upper_hbm, span_hbm, matrix_hbm, twiddle_hbm, fbuf,
     src, sbuf, rbuf, ure, uim, spec, matrix, twiddle, lower, upper, span,
-    coef, splats, kbuf, own_products, groups, abuf, wbuf, gbuf, gin, chain, alone, factors,
+    coef, splats, kbuf, own_products, groups, abuf, wbuf, gbuf, gin, chain, alone, factors, known,
     raw, gz, zrecv, obuf,
     load_sem, send_sem, recv_sem, arrived, cxr_sem, czr_sem, near_sem, far_sem,
 ):
@@ -415,6 +416,25 @@
     h_in = gin[1, xi]
     scale = 1.0 / (g_end + h_in * factors[2, ROWS - 1])
 
+    for part in range(2):
+        y = entering[0][part]
+        for i in range(ROWS):
+            y = factors[0, i] * y - factors[1, i] * rhs(i, part)
+            known[part, i] = y
+    reply = pre
+    for i in range(ROWS):
+        reply = factors[0, i] * reply
+        known[2, i] = reply
+    last_factor = factors[2, ROWS - 1]
+    state = [(last_factor * entering[1][part] + known[part, ROWS - 1]) * scale for part in range(2)]
+    state += [known[2, ROWS - 1] * scale, last_factor * scale * post]
+    for i in range(ROWS - 1, -1, -1):
+        if i < ROWS - 1:
+            e = factors[2, i]
+            state = [e * state[n] + known[n, i] for n in range(3)] + [e * state[3]]
+        for n in range(4):
+            known[n, i] = state[n]
+
     sy = [jnp.zeros_like(one)] * 2
     sz = [jnp.zeros_like(one)] * 2
     wait_for(zrecv.at[pl.ds(0, NZ - 1)], recv_sem.at[1])
@@ -428,25 +448,13 @@
             sy[part] = sy[part] + wy * v
             sz[part] = sz[part] + wz * v
 
-    ends = [[], []]
-    for part in range(2):
-        y = entering[0][part] + pre * sy[part]
-        for i in range(ROWS):
-            y = factors[0, i] * y - factors[1, i] * rhs(i, part)
-            ends[part].append(y)
-    solved = []
-    for part in range(2):
-        z_in = entering[1][part] + post * sz[part]
-        solved.append((factors[2, ROWS - 1] * z_in + ends[part][-1]) * scale)
-
     for o in (1, 0):
-        for i in range(8 * o + 7, 8 * o - 1, -1):
+        for i in range(8 * o, 8 * o + 8):
             for part, ref in enumerate((ure, uim)):
-                if i < ROWS - 1:
-                    solved[part] = factors[2, i] * solved[part] + ends[part][i]
+                x = known[part, i] + (known[2, i] * sy[part] + known[3, i] * sz[part])
                 for h in range(2):
                     at = o * 128 + h * 64 + (i % 8) * 8
-                    ref[at : at + 8, :] = solved[part][8 * h : 8 * h + 8, :]
+                    ref[at : at + 8, :] = x[8 * h : 8 * h + 8, :]
         rows = slice(128 * o, 128 * o + 128)
         back = product(jnp.concatenate([uim[rows, :], ure[rows, :]], axis=1), matrix[...])
         uim[rows, :] = back[:, :LANES]
@@ -477,9 +485,17 @@
         wait_for_octet(fbuf, arrived.at[2 + o])
 
 
-def assemble(fbuf, out):
-    for q in range(PLANES):
-        out[pl.ds(q, 4 * ROWS, stride=PLANES), :] = fbuf[q]
+def assemble(fbuf, out, held, sem):
+    count = 4 * ROWS // PARTS
+    copies = []
+    for n in range(PARTS):
+        for q in range(PLANES):
+            held[pl.ds(n * count * PLANES + q, count, stride=PLANES), :] = fbuf[q, n * count : (n + 1) * count, :]
+        rows = pl.ds(n * count * PLANES, count * PLANES)
+        copies.append(pltpu.make_async_copy(held.at[rows], out.at[rows], sem.at[n]))
+        copies[-1].start()
+    for copy in copies:
+        copy.wait()
 
 
 def local(source, lower, upper, span):
@@ -504,7 +520,7 @@
             vmem(BLOCKS, 1, LANES), vmem(4 * ROWS, 8, LANES), vmem(RADIX, LANES), vmem(5, 8 * RADIX, LANES),
             vmem(NZ, 5, RADIX, LANES), vmem(2, NXP, RADIX, LANES), vmem(NZ, RADIX, LANES),
             vmem(2, RADIX, LANES), vmem(2, NXP, RADIX, LANES), vmem(4, 4, RADIX, LANES),
-            vmem(4, ROWS, RADIX, LANES), vmem(3, ROWS, RADIX, LANES),
+            vmem(4, ROWS, RADIX, LANES), vmem(3, ROWS, RADIX, LANES), vmem(4, ROWS, RADIX, LANES),
             vmem(NXP, 64, LANES), vmem(2, 32, LANES), vmem(NZ, 32, LANES), vmem(PLANES, 64, LANES),
             dma((6,)), dma((6,)), dma((2,)), dma((4,)), dma((NXP,)), dma((NZ,)),
             pltpu.SemaphoreType.REGULAR, pltpu.SemaphoreType.REGULAR,
@@ -517,7 +533,8 @@
         assemble,
         out_shape=jax.ShapeDtypeStruct((ROWS * 4 * PLANES, LANES), f32),
         in_specs=[pl.BlockSpec(memory_space=pltpu.VMEM)],
-        out_specs=pl.BlockSpec(memory_space=pltpu.VMEM),
+        out_specs=pl.BlockSpec(memory_space=pltpu.HBM),
+        scratch_shapes=[vmem(ROWS * 4 * PLANES, LANES), dma((PARTS,))],
         compiler_params=pltpu.CompilerParams(vmem_limit_bytes=4 * 1024 * 1024),
     )(planes)
     result = result.reshape(ROWS, 2, 2, PLANES, LANES)

time: 30.1 us -> 30 us (level)
  no operation moved by 1% of the time
where the time goes in v5:
time: 30 us; the launch traced here: 29.9 us
  Pallas kernels  29.9 us (100%)
    pallas_call x1, Pallas kernels, local(): pl.pallas_call(kernel, out_shape=jax.ShapeDtypeStruct((PLANES, 64, LANES)...  29.2 us
    pallas_call x1, Pallas kernels, local(): pl.pallas_call(assemble, out_shape=jax.ShapeDtypeStruct((ROWS * 4 * PLANE...  0.74 us

profile of v5, /device:TPU:1, one launch (start us, length us, event | category | flops | bytes accessed | tf_op | source)
XLA Modules:
  0.0 29.9 jit_solution(3832491085337818774)
XLA Ops:
  0.0 29.2 %shard_map.64.fbuf = f32[8,64,128]{2,1,0:T(8,128)S(1)} custom-call(f32[512,128]{1,0:T(8,128)} %bitcast.10, f32[16]{0:T(128)} %lower_hbm.1, f32[16]{0:T(128)} %upper_hbm.1, f32[8]{0:T(128)} %span_hbm.1, bf16[1536,256]{1,0:T(8,128)(2,1)} %constant.4.clone.matrix_hbm, f32[32,128]{1,0:T(8,128)} %constant.5.clone.twiddle_hbm), custom_call_target="tpu_custom_call" | custom-call | tf_op jit(solution)/shard_map/pallas_call | solution.py:510
  29.2 0.7 %shard_map.65 = f32[512,128]{1,0:T(8,128)} custom-call(f32[8,64,128]{2,1,0:T(8,128)S(1)} %shard_map.64.fbuf), custom_call_target="tpu_custom_call" | custom-call | tf_op jit(solution)/shard_map/pallas_call | solution.py:532

commit v6 on v5

--- a/solution.py
+++ b/solution.py
@@ -102,7 +102,7 @@
     src, sbuf, rbuf, ure, uim, spec, matrix, twiddle, lower, upper, span,
     coef, splats, kbuf, own_products, groups, abuf, wbuf, gbuf, gin, chain, alone, factors, known,
     raw, gz, zrecv, obuf,
-    load_sem, send_sem, recv_sem, arrived, cxr_sem, czr_sem, near_sem, far_sem,
+    load_sem, send_sem, crossed, arrived, cxr_sem, czr_sem, near_sem, far_sem,
 ):
     gx = lax.axis_index("gx")
     gy = lax.axis_index("gy")
@@ -282,16 +282,22 @@
         at = [(i // 8) * 128 + h * 64 + (i % 8) * 8 for h in range(2)]
         return jnp.concatenate([spec[n : n + 8, lanes] for n in at], axis=0)
 
-    for way, order in enumerate((range(ROWS), range(ROWS - 1, -1, -1))):
-        for part in range(2):
-            y = None
-            for i in order:
-                r = rhs(i, part) * alone[2 * way + 1, i]
-                y = -r if y is None else alone[2 * way, i] * y - r
-            raw[xi, (2 * way + part) * RADIX : (2 * way + part + 1) * RADIX, :] = y
-    to_x = [remote(raw.at[xi], raw.at[xi], send_sem.at[3], recv_sem.at[0], at_x(q)) for q in x_peers]
-    for copy in to_x:
-        copy.start()
+    def half(ref, q, h, rows):
+        return ref.at[q, pl.ds(h * rows, rows)]
+
+    for h in range(2):
+        part_modes = slice(8 * h, 8 * h + 8)
+        for way, order in enumerate((range(ROWS), range(ROWS - 1, -1, -1))):
+            for part in range(2):
+                y = None
+                for i in order:
+                    at = (i // 8) * 128 + h * 64 + (i % 8) * 8
+                    r = spec[at : at + 8, part * LANES : (part + 1) * LANES] * alone[2 * way + 1, i, part_modes, :]
+                    y = -r if y is None else alone[2 * way, i, part_modes, :] * y - r
+                at = h * 32 + (2 * way + part) * 8
+                raw[xi, at : at + 8, :] = y
+        for q in x_peers:
+            remote(half(raw, xi, h, 32), half(raw, xi, h, 32), send_sem.at[3], crossed.at[h], at_x(q)).start()
 
     for slot in range(4):
         for k in range(4):
@@ -357,29 +363,30 @@
             abuf[way, t] = mirrored(scale * inv)
             enter[way] = (a * g + b) * inv
 
-    wait_for(raw.at[pl.ds(0, NXP - 1)], recv_sem.at[0])
-    entering = []
-    for way, order in enumerate((range(NXP), range(NXP - 1, -1, -1))):
-        run, mine = [jnp.zeros_like(one)] * 2, [jnp.zeros_like(one)] * 2
-        for j in order:
-            here = xi == j
-            a = abuf[way, j]
-            ae = a * (1.0 - gin[way, j])
+    entering = [[[], []], [[], []]]
+    for h in range(2):
+        part_modes = slice(8 * h, 8 * h + 8)
+        wait_for(raw.at[pl.ds(0, NXP - 1), pl.ds(0, 32)], crossed.at[h])
+        for way, order in enumerate((range(NXP), range(NXP - 1, -1, -1))):
+            none = jnp.zeros((8, LANES), jnp.float32)
+            run, mine = [none] * 2, [none] * 2
+            for j in order:
+                here = xi == j
+                a = abuf[way, j, part_modes, :]
+                ae = a * (1.0 - gin[way, j, part_modes, :])
+                for part in range(2):
+                    end, start = [raw[j, n : n + 8, :] for n in (
+                        h * 32 + (2 * way + part) * 8, h * 32 + (2 - 2 * way + part) * 8)]
+                    mine[part] = jnp.where(here, run[part], mine[part])
+                    run[part] = a * run[part] + (end + ae * start)
             for part in range(2):
-                end = raw[j, (2 * way + part) * RADIX : (2 * way + part + 1) * RADIX, :]
-                start = raw[j, (2 - 2 * way + part) * RADIX : (3 - 2 * way + part) * RADIX, :]
-                mine[part] = jnp.where(here, run[part], mine[part])
-                run[part] = a * run[part] + (end + ae * start)
-        for part in range(2):
-            gz[way, part * RADIX : (part + 1) * RADIX, :] = run[part]
-        entering.append(mine)
-
-    to_z = []
-    for q in z_peers:
-        which = jnp.where(q > zi, 0, 1)
-        to_z.append(remote(gz.at[which], zrecv.at[zi], send_sem.at[4], recv_sem.at[1], at_z(q)))
-    for copy in to_z:
-        copy.start()
+                at = h * 16 + part * 8
+                gz[way, at : at + 8, :] = run[part]
+                entering[way][part].append(mine[part])
+        for q in z_peers:
+            which = jnp.where(q > zi, 0, 1)
+            remote(half(gz, which, h, 16), half(zrecv, zi, h, 16), send_sem.at[4], crossed.at[2 + h], at_z(q)).start()
+    entering = [[jnp.concatenate(halves, axis=0) for halves in way] for way in entering]
 
     gbuf[...] = jnp.zeros_like(gbuf)
 
@@ -435,18 +442,23 @@
         for n in range(4):
             known[n, i] = state[n]
 
-    sy = [jnp.zeros_like(one)] * 2
-    sz = [jnp.zeros_like(one)] * 2
-    wait_for(zrecv.at[pl.ds(0, NZ - 1)], recv_sem.at[1])
-    for q in z_peers:
-        lower_side = q < zi
-        w = wbuf[q]
-        wy = jnp.where(lower_side, w, 0.0)
-        wz = jnp.where(lower_side, 0.0, w)
-        for part in range(2):
-            v = zrecv[q, part * RADIX : (part + 1) * RADIX, :]
-            sy[part] = sy[part] + wy * v
-            sz[part] = sz[part] + wz * v
+    brought = [[], []]
+    for h in range(2):
+        wait_for(zrecv.at[pl.ds(0, NZ - 1), pl.ds(0, 16)], crossed.at[2 + h])
+        none = jnp.zeros((8, LANES), jnp.float32)
+        sums = [[none] * 2, [none] * 2]
+        for q in z_peers:
+            lower_side = q < zi
+            w = wbuf[q, 8 * h : 8 * h + 8, :]
+            wy = jnp.where(lower_side, w, 0.0)
+            wz = jnp.where(lower_side, 0.0, w)
+            for part in range(2):
+                v = zrecv[q, h * 16 + part * 8 : h * 16 + part * 8 + 8, :]
+                sums[0][part] = sums[0][part] + wy * v
+                sums[1][part] = sums[1][part] + wz * v
+        brought[0].append(sums[0])
+        brought[1].append(sums[1])
+    sy, sz = [[jnp.concatenate([side[0][part], side[1][part]], axis=0) for part in range(2)] for side in brought]
 
     for o in (1, 0):
         for i in range(8 * o, 8 * o + 8):
@@ -522,7 +534,7 @@
             vmem(2, RADIX, LANES), vmem(2, NXP, RADIX, LANES), vmem(4, 4, RADIX, LANES),
             vmem(4, ROWS, RADIX, LANES), vmem(3, ROWS, RADIX, LANES), vmem(4, ROWS, RADIX, LANES),
             vmem(NXP, 64, LANES), vmem(2, 32, LANES), vmem(NZ, 32, LANES), vmem(PLANES, 64, LANES),
-            dma((6,)), dma((6,)), dma((2,)), dma((4,)), dma((NXP,)), dma((NZ,)),
+            dma((6,)), dma((6,)), dma((4,)), dma((4,)), dma((NXP,)), dma((NZ,)),
             pltpu.SemaphoreType.REGULAR, pltpu.SemaphoreType.REGULAR,
         ],
         compiler_params=pltpu.CompilerParams(

time: 30 us -> 29.8 us (level)
  no operation moved by 1% of the time
where the time goes in v6:
time: 29.8 us; the launch traced here: 29.7 us
  Pallas kernels  29.7 us (100%)
    pallas_call x1, Pallas kernels, local(): pl.pallas_call(kernel, out_shape=jax.ShapeDtypeStruct((PLANES, 64, LANES)...  29 us
    pallas_call x1, Pallas kernels, local(): pl.pallas_call(assemble, out_shape=jax.ShapeDtypeStruct((ROWS * 4 * PLANE...  0.74 us

profile of v6, /device:TPU:1, one launch (start us, length us, event | category | flops | bytes accessed | tf_op | source)
XLA Modules:
  0.0 29.7 jit_solution(12497798689517703260)
XLA Ops:
  0.0 29.0 %shard_map.64.fbuf = f32[8,64,128]{2,1,0:T(8,128)S(1)} custom-call(f32[512,128]{1,0:T(8,128)} %bitcast.10, f32[16]{0:T(128)} %lower_hbm.1, f32[16]{0:T(128)} %upper_hbm.1, f32[8]{0:T(128)} %span_hbm.1, bf16[1536,256]{1,0:T(8,128)(2,1)} %constant.4.clone.matrix_hbm, f32[32,128]{1,0:T(8,128)} %constant.5.clone.twiddle_hbm), custom_call_target="tpu_custom_call" | custom-call | tf_op jit(solution)/shard_map/pallas_call | solution.py:522
  29.0 0.7 %shard_map.65 = f32[512,128]{1,0:T(8,128)} custom-call(f32[8,64,128]{2,1,0:T(8,128)S(1)} %shard_map.64.fbuf), custom_call_target="tpu_custom_call" | custom-call | tf_op jit(solution)/shard_map/pallas_call | solution.py:544

commit v7 on v6

--- a/solution.py
+++ b/solution.py
@@ -100,7 +100,7 @@
 def kernel(
     source, lower_hbm, upper_hbm, span_hbm, matrix_hbm, twiddle_hbm, fbuf,
     src, sbuf, rbuf, ure, uim, spec, matrix, twiddle, lower, upper, span,
-    coef, splats, kbuf, own_products, groups, abuf, wbuf, gbuf, gin, chain, alone, factors, known,
+    coef, splats, kbuf, own_products, groups, abuf, wbuf, gbuf, gin, chain, alone, weights, factors, known,
     raw, gz, zrecv, obuf,
     load_sem, send_sem, crossed, arrived, cxr_sem, czr_sem, near_sem, far_sem,
 ):
@@ -127,7 +127,7 @@
 
     z_near = [lax.rem(zi + d, NZ) for d in (1, NZ - 1)]
     z_far = [lax.rem(zi + d, NZ) for d in (2, NZ - 2)]
-    near = [at_z(q) for q in z_near] + [at_x(q) for q in x_peers] + [at_gx(q) for q in gx_peers]
+    near = [at_gx(q) for q in gx_peers] + [at_x(q) for q in x_peers] + [at_z(q) for q in z_near]
     loads = [pltpu.make_async_copy(there, here, load_sem.at[n]) for n, (there, here) in enumerate((
         (source, src), (lower_hbm, lower), (upper_hbm, upper), (span_hbm, span),
         (twiddle_hbm, twiddle), (matrix_hbm, matrix)))]
@@ -204,6 +204,11 @@
 
     pivots(range(ROWS), low, upp, one, alone, 0)
     pivots(range(ROWS - 1, -1, -1), upp, low, one, alone, 2)
+    for way, order in enumerate((range(ROWS - 1, -1, -1), range(ROWS))):
+        run = -one
+        for i in order:
+            weights[way, i] = run * alone[2 * way + 1, i]
+            run = run * alone[2 * way, i]
 
     pl.semaphore_wait(near_sem, 2)
     for q in z_far:
@@ -260,6 +265,7 @@
     def wait_for_octet(ref, sem):
         wait_for(ref.at[pl.ds(0, PLANES - 1), pl.ds(0, 32)], sem)
 
+    alone_ends = [[None] * 2, [None] * 2]
     for o in range(2):
         wait_for_octet(rbuf, arrived.at[o])
         if o == 0:
@@ -275,7 +281,16 @@
             ure[transposed(o, k), :] = re * c + im * s
             uim[transposed(o, k), :] = im * c - re * s
         rows = slice(128 * o, 128 * o + 128)
-        spec[rows, :] = product(jnp.concatenate([ure[rows, :], uim[rows, :]], axis=1), matrix[...])
+        result = product(jnp.concatenate([ure[rows, :], uim[rows, :]], axis=1), matrix[...])
+        spec[rows, :] = result
+        for part in range(2):
+            lanes = slice(part * LANES, (part + 1) * LANES)
+            for i in range(8):
+                r = jnp.concatenate([result[h * 64 + i * 8 : h * 64 + i * 8 + 8, lanes] for h in range(2)], axis=0)
+                for way in range(2):
+                    share = weights[way, 8 * o + i] * r
+                    now = alone_ends[way][part]
+                    alone_ends[way][part] = share if now is None else now + share
 
     def rhs(i, part):
         lanes = slice(part * LANES, (part + 1) * LANES)
@@ -286,16 +301,10 @@
         return ref.at[q, pl.ds(h * rows, rows)]
 
     for h in range(2):
-        part_modes = slice(8 * h, 8 * h + 8)
-        for way, order in enumerate((range(ROWS), range(ROWS - 1, -1, -1))):
+        for way in range(2):
             for part in range(2):
-                y = None
-                for i in order:
-                    at = (i // 8) * 128 + h * 64 + (i % 8) * 8
-                    r = spec[at : at + 8, part * LANES : (part + 1) * LANES] * alone[2 * way + 1, i, part_modes, :]
-                    y = -r if y is None else alone[2 * way, i, part_modes, :] * y - r
                 at = h * 32 + (2 * way + part) * 8
-                raw[xi, at : at + 8, :] = y
+                raw[xi, at : at + 8, :] = alone_ends[way][part][8 * h : 8 * h + 8, :]
         for q in x_peers:
             remote(half(raw, xi, h, 32), half(raw, xi, h, 32), send_sem.at[3], crossed.at[h], at_x(q)).start()
 
@@ -460,17 +469,16 @@
         brought[1].append(sums[1])
     sy, sz = [[jnp.concatenate([side[0][part], side[1][part]], axis=0) for part in range(2)] for side in brought]
 
-    for o in (1, 0):
-        for i in range(8 * o, 8 * o + 8):
-            for part, ref in enumerate((ure, uim)):
-                x = known[part, i] + (known[2, i] * sy[part] + known[3, i] * sz[part])
-                for h in range(2):
-                    at = o * 128 + h * 64 + (i % 8) * 8
-                    ref[at : at + 8, :] = x[8 * h : 8 * h + 8, :]
-        rows = slice(128 * o, 128 * o + 128)
-        back = product(jnp.concatenate([uim[rows, :], ure[rows, :]], axis=1), matrix[...])
-        uim[rows, :] = back[:, :LANES]
-        ure[rows, :] = back[:, LANES:]
+    for i in range(ROWS):
+        for part, ref in enumerate((ure, uim)):
+            x = known[part, i] + (known[2, i] * sy[part] + known[3, i] * sz[part])
+            for h in range(2):
+                at = (i // 8) * 128 + h * 64 + (i % 8) * 8
+                ref[at : at + 8, :] = x[8 * h : 8 * h + 8, :]
+    back = product(jnp.concatenate([uim[...], ure[...]], axis=1), matrix[...])
+    uim[...] = back[:, :LANES]
+    ure[...] = back[:, LANES:]
+    for o in range(2):
         values = []
         for k in range(RADIX):
             re = ure[transposed(o, k), :]
@@ -532,7 +540,8 @@
             vmem(BLOCKS, 1, LANES), vmem(4 * ROWS, 8, LANES), vmem(RADIX, LANES), vmem(5, 8 * RADIX, LANES),
             vmem(NZ, 5, RADIX, LANES), vmem(2, NXP, RADIX, LANES), vmem(NZ, RADIX, LANES),
             vmem(2, RADIX, LANES), vmem(2, NXP, RADIX, LANES), vmem(4, 4, RADIX, LANES),
-            vmem(4, ROWS, RADIX, LANES), vmem(3, ROWS, RADIX, LANES), vmem(4, ROWS, RADIX, LANES),
+            vmem(4, ROWS, RADIX, LANES), vmem(2, ROWS, RADIX, LANES), vmem(3, ROWS, RADIX, LANES),
+            vmem(4, ROWS, RADIX, LANES),
             vmem(NXP, 64, LANES), vmem(2, 32, LANES), vmem(NZ, 32, LANES), vmem(PLANES, 64, LANES),
             dma((6,)), dma((6,)), dma((4,)), dma((4,)), dma((NXP,)), dma((NZ,)),
             pltpu.SemaphoreType.REGULAR, pltpu.SemaphoreType.REGULAR,

time: 29.8 us -> 29.8 us (level)
  no operation moved by 1% of the time
where the time goes in v7:
time: 29.8 us; the launch traced here: 29.7 us
  Pallas kernels  29.7 us (100%)
    pallas_call x1, Pallas kernels, local(): pl.pallas_call(kernel, out_shape=jax.ShapeDtypeStruct((PLANES, 64, LANES)...  29 us
    pallas_call x1, Pallas kernels, local(): pl.pallas_call(assemble, out_shape=jax.ShapeDtypeStruct((ROWS * 4 * PLANE...  0.74 us

profile of v7, /device:TPU:1, one launch (start us, length us, event | category | flops | bytes accessed | tf_op | source)
XLA Modules:
  0.0 29.7 jit_solution(8326704240281376342)
XLA Ops:
  0.0 29.0 %shard_map.64.fbuf = f32[8,64,128]{2,1,0:T(8,128)S(1)} custom-call(f32[512,128]{1,0:T(8,128)} %bitcast.10, f32[16]{0:T(128)} %lower_hbm.1, f32[16]{0:T(128)} %upper_hbm.1, f32[8]{0:T(128)} %span_hbm.1, bf16[1536,256]{1,0:T(8,128)(2,1)} %constant.4.clone.matrix_hbm, f32[32,128]{1,0:T(8,128)} %constant.5.clone.twiddle_hbm), custom_call_target="tpu_custom_call" | custom-call | tf_op jit(solution)/shard_map/pallas_call | solution.py:530
  29.0 0.7 %shard_map.65 = f32[512,128]{1,0:T(8,128)} custom-call(f32[8,64,128]{2,1,0:T(8,128)S(1)} %shard_map.64.fbuf), custom_call_target="tpu_custom_call" | custom-call | tf_op jit(solution)/shard_map/pallas_call | solution.py:553

commit v8 on v7

--- a/solution.py
+++ b/solution.py
@@ -141,23 +141,6 @@
     loads[0].wait()
     for q in range(PLANES):
         sbuf[q] = src[pl.ds(q, 4 * ROWS, stride=PLANES), :]
-
-    pl.semaphore_wait(barrier, len(near))
-
-    def remote(src_ref, dst_ref, send, recv, device):
-        return pltpu.make_async_remote_copy(
-            src_ref=src_ref, dst_ref=dst_ref, send_sem=send, recv_sem=recv,
-            device_id=device, device_id_type=MESH)
-
-    def octet(ref, q, o):
-        return ref.at[q, pl.ds(32 * o, 32)]
-
-    for o in range(2):
-        for q in gx_peers:
-            remote(octet(sbuf, q, o), octet(rbuf, gx, o), send_sem.at[0], arrived.at[o], at_gx(q)).start()
-    for q in z_near:
-        pl.semaphore_signal(near_sem, inc=1, device_id=at_z(q), device_id_type=MESH)
-    rbuf[gx] = sbuf[gx]
 
     for load in loads[1:4]:
         load.wait()
@@ -178,9 +161,28 @@
         row = jnp.where(lane == i, value, row)
     coef[gy] = row
 
+    pl.semaphore_wait(barrier, len(near))
+
+    def remote(src_ref, dst_ref, send, recv, device):
+        return pltpu.make_async_remote_copy(
+            src_ref=src_ref, dst_ref=dst_ref, send_sem=send, recv_sem=recv,
+            device_id=device, device_id_type=MESH)
+
     coef_x = [remote(coef.at[gy], coef.at[gy], send_sem.at[1], cxr_sem.at[xi], at_x(q)) for q in x_peers]
     for copy in coef_x:
         copy.start()
+
+    for q in z_near:
+        pl.semaphore_signal(near_sem, inc=1, device_id=at_z(q), device_id_type=MESH)
+
+    def octet(ref, q, o):
+        return ref.at[q, pl.ds(32 * o, 32)]
+
+    for o in range(2):
+        for q in gx_peers:
+            remote(octet(sbuf, q, o), octet(rbuf, gx, o), send_sem.at[0], arrived.at[o], at_gx(q)).start()
+    rbuf[gx] = sbuf[gx]
+
 
     k1 = lax.broadcasted_iota(jnp.int32, (RADIX, LANES), 0)
     k2 = lax.broadcasted_iota(jnp.int32, (RADIX, LANES), 1)
@@ -225,7 +227,7 @@
 
     kbuf[...] = kappa
 
-    def block_products(blocks, ways, finish):
+    def block_products(blocks, ways, finish, modes=None):
         rows = jnp.concatenate([coef[t] for t in blocks], axis=0)
         sub = lax.broadcasted_iota(jnp.int32, (8, LANES), 0)
         turn = jnp.where(sub < NXP, ways[0], ways[1]) == 1
@@ -236,12 +238,17 @@
             splats[k] = one
             if k < ROWS:
                 scale = one if scale is None else scale * one
-        for k in range(0, HALF, 3):
-            waves = [jnp.broadcast_to(kbuf[n : n + 1, :], (8, LANES)) for n in range(k, k + 3)]
-            state = [None] * 3
+        for group in modes or [[(n, n) for n in range(k, k + 3)] for k in range(0, HALF, 3)]:
+            waves = []
+            for n, m in group:
+                waves.append(jnp.broadcast_to(kbuf[n : n + 1, :], (8, LANES)))
+                if m != n:
+                    other = jnp.broadcast_to(kbuf[m : m + 1, :], (8, LANES))
+                    waves[-1] = jnp.where(sub < NXP, waves[-1], other)
+            state = [None] * len(group)
             for i in range(ROWS):
                 l, u, total, gained = [splats[n * ROWS + i] for n in range(4)]
-                for n in range(3):
+                for n in range(len(group)):
                     rounded = ((total + waves[n]) - total) + gained
                     if i == 0:
                         state[n] = (l, rounded, l, u + rounded)
@@ -250,12 +257,12 @@
                     a = l * a + rounded * c
                     b = l * b + rounded * d
                     state[n] = (a, b, a + u * c, b + u * d)
-            for n in range(3):
-                finish(k + n, scaled(state[n] + (scale,)))
-
-    def keep_own(k, values):
+            for n, parts in enumerate(group):
+                finish(parts, scaled(state[n] + (scale,)))
+
+    def keep_own(parts, values):
         for n, v in enumerate(values):
-            own_products[n, 8 * k : 8 * k + 8, :] = v
+            own_products[n, 8 * parts[0] : 8 * parts[0] + 8, :] = v
 
     block_products([base + j for j in range(NXP)] * 2, (0, 1), keep_own)
 
@@ -315,48 +322,51 @@
     def next_block(x, shift):
         return tuple(pltpu.roll(v, 8 - shift, 0) for v in x)
 
-    @pl.loop(0, NZ // 2)
-    def _(n):
-        pair = (lax.rem(zi + n + 1, NZ), lax.rem(zi + NZ - 1 - n, NZ))
-        ways = [(q > zi).astype(jnp.int32) for q in pair]
-
-        def arrive(q):
-            there = coef.at[pl.ds(q * NXP, NXP)]
-            remote(there, there, send_sem.at[2], czr_sem.at[q], at_z(q)).wait_recv()
-
-        arrive(pair[0])
-
-        @pl.when(n < NZ // 2 - 1)
-        def _():
-            arrive(pair[1])
-
-        def keep_groups(k, values):
+    def arrive(q):
+        there = coef.at[pl.ds(q * NXP, NXP)]
+        remote(there, there, send_sem.at[2], czr_sem.at[q], at_z(q)).wait_recv()
+
+    def keep_groups(pair):
+        def keep(parts, values):
             for shift in (1, 2):
                 later = next_block(values, shift)
                 values = times(later[:4], values[:4]) + (later[4] * values[4],)
             values = scaled(values)
             for m, v in enumerate(values):
                 for g in range(2):
-                    groups[pair[g], m, k : k + 1, :] = v[NXP * g : NXP * g + 1, :]
-
-        blocks = [q * NXP + jnp.where(w == 0, j, NXP - 1 - j) for q, w in zip(pair, ways) for j in range(NXP)]
-        block_products(blocks, ways, keep_groups)
-
-        def join(g):
-            far = ways[g] != 1 - g
-            slot = ways[g] + 2 * far.astype(jnp.int32)
-            whole = tuple(groups[pair[g], k] for k in range(4))
-            old = tuple(chain[slot, k] for k in range(4))
-            outer = tuple(jnp.where(far, w, o) for w, o in zip(whole, old))
-            inner = tuple(jnp.where(far, o, w) for w, o in zip(whole, old))
-            for k, v in enumerate(scaled(times(outer, inner))):
-                chain[slot, k] = v
-
-        join(0)
-
-        @pl.when(n < NZ // 2 - 1)
-        def _():
-            join(1)
+                    groups[pair[g], m, parts[g] : parts[g] + 1, :] = v[NXP * g : NXP * g + 1, :]
+
+        return keep
+
+    def join(q, way, upward):
+        far = way != int(upward)
+        slot = way + 2 * far.astype(jnp.int32)
+        whole = tuple(groups[q, k] for k in range(4))
+        old = tuple(chain[slot, k] for k in range(4))
+        outer = tuple(jnp.where(far, w, o) for w, o in zip(whole, old))
+        inner = tuple(jnp.where(far, o, w) for w, o in zip(whole, old))
+        for k, v in enumerate(scaled(times(outer, inner))):
+            chain[slot, k] = v
+
+    def in_order(q, way):
+        return [q * NXP + jnp.where(way == 0, j, NXP - 1 - j) for j in range(NXP)]
+
+    @pl.loop(0, NZ // 2 - 1)
+    def _(n):
+        pair = (lax.rem(zi + n + 1, NZ), lax.rem(zi + NZ - 1 - n, NZ))
+        ways = [(q > zi).astype(jnp.int32) for q in pair]
+        for q in pair:
+            arrive(q)
+        block_products(in_order(pair[0], ways[0]) + in_order(pair[1], ways[1]), ways, keep_groups(pair))
+        for q, way, upward in zip(pair, ways, (True, False)):
+            join(q, way, upward)
+
+    across = lax.rem(zi + NZ // 2, NZ)
+    way = (across > zi).astype(jnp.int32)
+    arrive(across)
+    block_products(in_order(across, way) * 2, (way, way), keep_groups((across, across)),
+                   [[(0, 5), (1, 6), (2, 7)], [(3, 8), (4, 4)]])
+    join(across, way, True)
 
     enter = []
     for way in range(2):
@@ -469,16 +479,17 @@
         brought[1].append(sums[1])
     sy, sz = [[jnp.concatenate([side[0][part], side[1][part]], axis=0) for part in range(2)] for side in brought]
 
-    for i in range(ROWS):
-        for part, ref in enumerate((ure, uim)):
-            x = known[part, i] + (known[2, i] * sy[part] + known[3, i] * sz[part])
-            for h in range(2):
-                at = (i // 8) * 128 + h * 64 + (i % 8) * 8
-                ref[at : at + 8, :] = x[8 * h : 8 * h + 8, :]
-    back = product(jnp.concatenate([uim[...], ure[...]], axis=1), matrix[...])
-    uim[...] = back[:, :LANES]
-    ure[...] = back[:, LANES:]
-    for o in range(2):
+    for o in (1, 0):
+        for i in range(8 * o, 8 * o + 8):
+            for part, ref in enumerate((ure, uim)):
+                x = known[part, i] + (known[2, i] * sy[part] + known[3, i] * sz[part])
+                for h in range(2):
+                    at = o * 128 + h * 64 + (i % 8) * 8
+                    ref[at : at + 8, :] = x[8 * h : 8 * h + 8, :]
+        rows = slice(128 * o, 128 * o + 128)
+        back = product(jnp.concatenate([uim[rows, :], ure[rows, :]], axis=1), matrix[...])
+        uim[rows, :] = back[:, :LANES]
+        ure[rows, :] = back[:, LANES:]
         values = []
         for k in range(RADIX):
             re = ure[transposed(o, k), :]

time: 29.8 us -> 29.8 us (level)
  no operation moved by 1% of the time
where the time goes in v8:
time: 29.8 us; the launch traced here: 29.7 us
  Pallas kernels  29.7 us (100%)
    pallas_call x1, Pallas kernels, local(): pl.pallas_call(kernel, out_shape=jax.ShapeDtypeStruct((PLANES, 64, LANES)...  29 us
    pallas_call x1, Pallas kernels, local(): pl.pallas_call(assemble, out_shape=jax.ShapeDtypeStruct((ROWS * 4 * PLANE...  0.74 us

profile of v8, /device:TPU:1, one launch (start us, length us, event | category | flops | bytes accessed | tf_op | source)
XLA Modules:
  0.0 29.7 jit_solution(11527687361938684232)
XLA Ops:
  0.0 29.0 %shard_map.64.fbuf = f32[8,64,128]{2,1,0:T(8,128)S(1)} custom-call(f32[512,128]{1,0:T(8,128)} %bitcast.10, f32[16]{0:T(128)} %lower_hbm.1, f32[16]{0:T(128)} %upper_hbm.1, f32[8]{0:T(128)} %span_hbm.1, bf16[1536,256]{1,0:T(8,128)(2,1)} %constant.4.clone.matrix_hbm, f32[32,128]{1,0:T(8,128)} %constant.5.clone.twiddle_hbm), custom_call_target="tpu_custom_call" | custom-call | tf_op jit(solution)/shard_map/pallas_call | solution.py:541
  29.0 0.7 %shard_map.65 = f32[512,128]{1,0:T(8,128)} custom-call(f32[8,64,128]{2,1,0:T(8,128)S(1)} %shard_map.64.fbuf), custom_call_target="tpu_custom_call" | custom-call | tf_op jit(solution)/shard_map/pallas_call | solution.py:564

commit v9 on v8

--- a/solution.py
+++ b/solution.py
@@ -178,9 +178,10 @@
     def octet(ref, q, o):
         return ref.at[q, pl.ds(32 * o, 32)]
 
-    for o in range(2):
-        for q in gx_peers:
-            remote(octet(sbuf, q, o), octet(rbuf, gx, o), send_sem.at[0], arrived.at[o], at_gx(q)).start()
+    for some in (gx_peers[:2], gx_peers[2:6], gx_peers[6:]):
+        for o in range(2):
+            for q in some:
+                remote(octet(sbuf, q, o), octet(rbuf, gx, o), send_sem.at[0], arrived.at[o], at_gx(q)).start()
     rbuf[gx] = sbuf[gx]
 
 
@@ -479,17 +480,19 @@
         brought[1].append(sums[1])
     sy, sz = [[jnp.concatenate([side[0][part], side[1][part]], axis=0) for part in range(2)] for side in brought]
 
-    for o in (1, 0):
-        for i in range(8 * o, 8 * o + 8):
-            for part, ref in enumerate((ure, uim)):
-                x = known[part, i] + (known[2, i] * sy[part] + known[3, i] * sz[part])
-                for h in range(2):
-                    at = o * 128 + h * 64 + (i % 8) * 8
-                    ref[at : at + 8, :] = x[8 * h : 8 * h + 8, :]
-        rows = slice(128 * o, 128 * o + 128)
-        back = product(jnp.concatenate([uim[rows, :], ure[rows, :]], axis=1), matrix[...])
-        uim[rows, :] = back[:, :LANES]
-        ure[rows, :] = back[:, LANES:]
+    def send_back(q, o):
+        remote(octet(obuf, q, o), octet(fbuf, gx, o), send_sem.at[5], arrived.at[2 + o], at_gx(q)).start()
+
+    for i in range(ROWS):
+        for part, ref in enumerate((ure, uim)):
+            x = known[part, i] + (known[2, i] * sy[part] + known[3, i] * sz[part])
+            for h in range(2):
+                at = (i // 8) * 128 + h * 64 + (i % 8) * 8
+                ref[at : at + 8, :] = x[8 * h : 8 * h + 8, :]
+    back = product(jnp.concatenate([uim[...], ure[...]], axis=1), matrix[...])
+    uim[...] = back[:, :LANES]
+    ure[...] = back[:, LANES:]
+    for o in range(2):
         values = []
         for k in range(RADIX):
             re = ure[transposed(o, k), :]
@@ -501,8 +504,11 @@
         for a in range(RADIX):
             for part in range(2):
                 obuf[a // 2, pl.ds(32 * o + 2 * part + a % 2, 8, stride=4), :] = values[a][part]
-        for q in gx_peers:
-            remote(octet(obuf, q, o), octet(fbuf, gx, o), send_sem.at[5], arrived.at[2 + o], at_gx(q)).start()
+        for q in gx_peers[:2]:
+            send_back(q, o)
+    for o in range(2):
+        for q in gx_peers[2:]:
+            send_back(q, o)
     own = pltpu.make_async_copy(obuf.at[gx], fbuf.at[gx], load_sem.at[0])
     own.start()
     wait_for(sbuf.at[pl.ds(0, PLANES - 1)], send_sem.at[0])

time: 29.8 us -> 29.5 us (0.990)
  Pallas kernels: 29.7 us -> 29.4 us
where the time goes in v9:
time: 29.5 us; the launch traced here: 29.4 us
  Pallas kernels  29.4 us (100%)
    pallas_call x1, Pallas kernels, local(): pl.pallas_call(kernel, out_shape=jax.ShapeDtypeStruct((PLANES, 64, LANES)...  28.7 us
    pallas_call x1, Pallas kernels, local(): pl.pallas_call(assemble, out_shape=jax.ShapeDtypeStruct((ROWS * 4 * PLANE...  0.74 us

profile of v9, /device:TPU:1, one launch (start us, length us, event | category | flops | bytes accessed | tf_op | source)
XLA Modules:
  0.0 29.4 jit_solution(834681498521031094)
XLA Ops:
  0.0 28.7 %shard_map.64.fbuf = f32[8,64,128]{2,1,0:T(8,128)S(1)} custom-call(f32[512,128]{1,0:T(8,128)} %bitcast.10, f32[16]{0:T(128)} %lower_hbm.1, f32[16]{0:T(128)} %upper_hbm.1, f32[8]{0:T(128)} %span_hbm.1, bf16[1536,256]{1,0:T(8,128)(2,1)} %constant.4.clone.matrix_hbm, f32[32,128]{1,0:T(8,128)} %constant.5.clone.twiddle_hbm), custom_call_target="tpu_custom_call" | custom-call | tf_op jit(solution)/shard_map/pallas_call | solution.py:547
  28.7 0.7 %shard_map.65 = f32[512,128]{1,0:T(8,128)} custom-call(f32[8,64,128]{2,1,0:T(8,128)S(1)} %shard_map.64.fbuf), custom_call_target="tpu_custom_call" | custom-call | tf_op jit(solution)/shard_map/pallas_call | solution.py:570

commit v10 on v9

--- a/solution.py
+++ b/solution.py
@@ -168,7 +168,10 @@
             src_ref=src_ref, dst_ref=dst_ref, send_sem=send, recv_sem=recv,
             device_id=device, device_id_type=MESH)
 
-    coef_x = [remote(coef.at[gy], coef.at[gy], send_sem.at[1], cxr_sem.at[xi], at_x(q)) for q in x_peers]
+    def wait_for(ref, sem):
+        pltpu.make_async_copy(ref, ref, sem).wait()
+
+    coef_x = [remote(coef.at[gy], coef.at[gy], send_sem.at[1], cxr_sem, at_x(q)) for q in x_peers]
     for copy in coef_x:
         copy.start()
 
@@ -217,9 +220,7 @@
     for q in z_far:
         pl.semaphore_signal(far_sem, inc=1, device_id=at_z(q), device_id_type=MESH)
 
-    for q in x_peers:
-        there = coef.at[base + q]
-        remote(there, there, send_sem.at[1], cxr_sem.at[q], at_x(q)).wait_recv()
+    wait_for(coef.at[pl.ds(0, NXP - 1)], cxr_sem)
     pl.semaphore_wait(far_sem, 2)
     group = coef.at[pl.ds(base, NXP)]
     coef_z = [remote(group, group, send_sem.at[2], czr_sem.at[zi], at_z(q)) for q in z_peers]
@@ -267,9 +268,6 @@
 
     block_products([base + j for j in range(NXP)] * 2, (0, 1), keep_own)
 
-    def wait_for(ref, sem):
-        pltpu.make_async_copy(ref, ref, sem).wait()
-
     def wait_for_octet(ref, sem):
         wait_for(ref.at[pl.ds(0, PLANES - 1), pl.ds(0, 32)], sem)
 
@@ -313,8 +311,10 @@
             for part in range(2):
                 at = h * 32 + (2 * way + part) * 8
                 raw[xi, at : at + 8, :] = alone_ends[way][part][8 * h : 8 * h + 8, :]
-        for q in x_peers:
-            remote(half(raw, xi, h, 32), half(raw, xi, h, 32), send_sem.at[3], crossed.at[h], at_x(q)).start()
+    for some in (x_peers[:1], x_peers[1:]):
+        for h in range(2):
+            for q in some:
+                remote(half(raw, xi, h, 32), half(raw, xi, h, 32), send_sem.at[3], crossed.at[h], at_x(q)).start()
 
     for slot in range(4):
         for k in range(4):
@@ -560,7 +560,7 @@
             vmem(4, ROWS, RADIX, LANES), vmem(2, ROWS, RADIX, LANES), vmem(3, ROWS, RADIX, LANES),
             vmem(4, ROWS, RADIX, LANES),
             vmem(NXP, 64, LANES), vmem(2, 32, LANES), vmem(NZ, 32, LANES), vmem(PLANES, 64, LANES),
-            dma((6,)), dma((6,)), dma((4,)), dma((4,)), dma((NXP,)), dma((NZ,)),
+            dma((6,)), dma((6,)), dma((4,)), dma((4,)), dma, dma((NZ,)),
             pltpu.SemaphoreType.REGULAR, pltpu.SemaphoreType.REGULAR,
         ],
         compiler_params=pltpu.CompilerParams(

time: 29.5 us -> 29.5 us (level)
  no operation moved by 1% of the time
where the time goes in v10:
time: 29.5 us; the launch traced here: 29.4 us
  Pallas kernels  29.4 us (100%)
    pallas_call x1, Pallas kernels, local(): pl.pallas_call(kernel, out_shape=jax.ShapeDtypeStruct((PLANES, 64, LANES)...  28.6 us
    pallas_call x1, Pallas kernels, local(): pl.pallas_call(assemble, out_shape=jax.ShapeDtypeStruct((ROWS * 4 * PLANE...  0.74 us

profile of v10, /device:TPU:1, one launch (start us, length us, event | category | flops | bytes accessed | tf_op | source)
XLA Modules:
  0.0 29.4 jit_solution(17739423201015281606)
XLA Ops:
  0.0 28.6 %shard_map.64.fbuf = f32[8,64,128]{2,1,0:T(8,128)S(1)} custom-call(f32[512,128]{1,0:T(8,128)} %bitcast.10, f32[16]{0:T(128)} %lower_hbm.1, f32[16]{0:T(128)} %upper_hbm.1, f32[8]{0:T(128)} %span_hbm.1, bf16[1536,256]{1,0:T(8,128)(2,1)} %constant.4.clone.matrix_hbm, f32[32,128]{1,0:T(8,128)} %constant.5.clone.twiddle_hbm), custom_call_target="tpu_custom_call" | custom-call | tf_op jit(solution)/shard_map/pallas_call | solution.py:547
  28.6 0.7 %shard_map.65 = f32[512,128]{1,0:T(8,128)} custom-call(f32[8,64,128]{2,1,0:T(8,128)S(1)} %shard_map.64.fbuf), custom_call_target="tpu_custom_call" | custom-call | tf_op jit(solution)/shard_map/pallas_call | solution.py:570
